TPU v7x, 256 devices: a whole 4x4x8 slice. The times are simulated.
256 devices in a mesh: gx: 8 (over z), gy: 16 (over y_lo, x, core), gz: 2 (over y_hi).
Axes of the slice: x: 4, y: 4 (y_hi: 2, y_lo: 2; y = y_hi * 2 + y_lo), z: 8, core: 2. Of those that a mesh axis runs over, the one named last changes fastest.
Arguments:
- plume_flow_variables: float32 [6, 64, 256, 256], P(None, 'gx', 'gy', 'gz'), may hold values from -6 to 6
- thermal_field: float32 [128, 128, 512], P(None, ('gx', 'gz'), 'gy'), may hold values from -6 to 6
- matter_condition: int32 [128, 128, 512], P(None, ('gx', 'gz'), 'gy'), may hold values from 0 to 2
- pool_boundary_level: int32 [64, 256], P('gx', 'gy'), may hold values from 0 to 127
- beam_focus_path: int32 [4, 2], replicated, may hold values from 0 to 511, as said below
Outputs:
- gas_out: float32 [6, 64, 256, 256], P(None, 'gx', 'gy', 'gz')
- temperature_out: float32 [128, 128, 512], P(None, ('gx', 'gz'), 'gy')
Inputs may be any that keep to these rules, and one draw needn't show every extreme that they name: `beam_focus_path`: column 0 is a position along the part's first lateral dimension, below 128; column 1 along the second, below 512.
All inputs are finite; a program needn't handle non-finite values.
Results may differ from a plain program's by a relative error of at most 0.0001.
Values sent between devices are 32-bit elements; how exact they have to be, the bound alone decides.
A program may use at most 64 MiB of HBM per device.

v0:
```python
import jax
import jax.numpy as jnp
from jax import lax
from jax.sharding import PartitionSpec as P

STEPS = 2
SUBSTEPS = 2


GAS_STEP = 0.3
DRIFT_SPEED = 0.5
VAPOR_LOAD = 0.3
AMBIENT_LOAD = 0.7
STIFFNESS = 1.0
VISCOSITY = (0.2, 0.1, 0.15, 0.15, 0.15, 0.2)
HEAT_STEP = 1.0
POWDER_COND = 0.04
SOLID_COND = 0.15
LIQUID_COND = 0.09
LASER_POWER = 3.0
SPOT_RADIUS = 6.0
ABSORB_DEPTH = 4.0
BOIL_LEVEL = 1.0
BACK_PRESSURE = 0.5
LATENT_HEAT = 0.3
VAPOR_SOURCE = 0.5
RECOIL_PUSH = 0.4
RECOIL_PRESSURE = 0.6


def padded_2(value, sides, width):
    for axis, dim in sides:
        size, length = (lax.axis_size(axis), value.shape[dim])
        up = [(i, (i + 1) % size) for i in range(size - 1)]
        down = [(j, i) for i, j in up]
        last = lax.slice_in_dim(value, length - width, length, axis=dim)
        leading = lax.slice_in_dim(value, 0, width, axis=dim)
        before = lax.ppermute(last, axis, up)
        after = lax.ppermute(leading, axis, down)
        value = jnp.concatenate([before, value, after], axis=dim)
    return value


def extended(value, sides, width):
    edges = {}
    for axis, dim in sides:
        size, length = (lax.axis_size(axis), value.shape[dim])
        up = [(i, (i + 1) % size) for i in range(size - 1)]
        last = lax.slice_in_dim(value, length - width, length, axis=dim)
        leading = lax.slice_in_dim(value, 0, width, axis=dim)
        edges[dim] = (
            lax.ppermute(last, axis, up),
            lax.ppermute(leading, axis, [(b, a) for a, b in up]),
        )
    done = []
    for _, dim in sides:
        low, high = edges[dim]
        around = [(width, width) if d in done else (0, 0) for d in range(value.ndim)]
        value = jnp.concatenate([jnp.pad(low, around), value, jnp.pad(high, around)], axis=dim)
        done.append(dim)
    return value


def broadcast(value, axis, root):
    return lax.dynamic_index_in_dim(lax.all_gather(value, axis), root, 0, keepdims=False)


def laid_out(blocks, dim):
    shape = list(blocks.shape[1:])
    shape[dim] *= blocks.shape[0]
    return jnp.moveaxis(blocks, 0, dim).reshape(shape)


def copy_for_each(value, axis):
    copies = jnp.broadcast_to(value, (lax.axis_size(axis), *value.shape))
    return lax.all_to_all(copies, axis, split_axis=0, concat_axis=0, tiled=True)


def gather_directly(value, axis, dim):
    return laid_out(copy_for_each(value, axis), dim)


def gas_rate(padded):
    center = padded[:, 1:-1, 1:-1, 1:-1]
    east_side = padded[:, 2:, 1:-1, 1:-1]
    west_side = padded[:, :-2, 1:-1, 1:-1]
    north_side = padded[:, 1:-1, 2:, 1:-1]
    south_side = padded[:, 1:-1, :-2, 1:-1]
    upper_side = padded[:, 1:-1, 1:-1, 2:]
    lower_side = padded[:, 1:-1, 1:-1, :-2]
    slope_x = 0.5 * (east_side - west_side)
    slope_y = 0.5 * (north_side - south_side)
    slope_z = 0.5 * (upper_side - lower_side)
    laplace = (
        east_side + west_side + north_side + south_side + upper_side + lower_side - 6.0 * center
    )
    spread = slope_x[2] + slope_y[3] + slope_z[4]
    viscous = jnp.array(VISCOSITY, jnp.float32).reshape(6, 1, 1, 1)
    coupled = jnp.stack(
        [
            -VAPOR_LOAD * spread,
            -AMBIENT_LOAD * spread,
            -slope_x[5],
            -slope_y[5],
            -slope_z[5],
            -STIFFNESS * spread,
        ]
    )
    return coupled - DRIFT_SPEED * slope_z + viscous * laplace


def neighbours(padded):
    return [
        padded[2:, 1:-1, 1:-1],
        padded[:-2, 1:-1, 1:-1],
        padded[1:-1, 2:, 1:-1],
        padded[1:-1, :-2, 1:-1],
        padded[1:-1, 1:-1, 2:],
        padded[1:-1, 1:-1, :-2],
    ]


def heat_rate(padded_temp, padded_cond):
    center = padded_temp[1:-1, 1:-1, 1:-1]
    cond_center = padded_cond[1:-1, 1:-1, 1:-1]
    total = jnp.zeros_like(center)
    for temp_side, cond_side in zip(neighbours(padded_temp), neighbours(padded_cond)):
        total = total + 0.5 * (cond_center + cond_side) * (temp_side - center)
    return total


def conductivity(matter_condition):
    return jnp.where(
        matter_condition == 0,
        POWDER_COND,
        jnp.where(matter_condition == 1, SOLID_COND, LIQUID_COND),
    ).astype(jnp.float32)


def laser_heat(x_cells, y_cells, depth_cells, target):
    along_x = jnp.exp(-(((x_cells - target[0].astype(jnp.float32)) / SPOT_RADIUS) ** 2))
    along_y = jnp.exp(-(((y_cells - target[1].astype(jnp.float32)) / SPOT_RADIUS) ** 2))
    along_depth = jnp.exp(-depth_cells / ABSORB_DEPTH)
    return (
        LASER_POWER * along_depth[:, None, None] * along_x[None, :, None] * along_y[None, None, :]
    )


def evaporation(surface_temp, pressure):
    return jax.nn.softplus(surface_temp - BOIL_LEVEL - BACK_PRESSURE * pressure)


def refine(values):
    return jnp.repeat(jnp.repeat(values, 2, axis=0), 2, axis=1)


def coarsen(values):
    rows, cols = values.shape
    return 0.25 * jnp.sum(values.reshape(rows // 2, 2, cols // 2, 2), axis=(1, 3))


def global_cells(start, count):
    return (start + jnp.arange(count, dtype=jnp.int32)).astype(jnp.float32)


def valid_cycle(position, devices, count):
    global_index = position * count - 1 + jnp.arange(count + 2, dtype=jnp.int32)
    return ((global_index >= 0) & (global_index < count * devices)).astype(jnp.float32)


def advance(vapor_state):
    padded = padded_2(vapor_state, (("gx", 1), ("gy", 2), ("gz", 3)), 2)
    first_section = padded[:, 1:-1, 1:-1, 1:-1] + GAS_STEP * gas_rate(padded)
    inside_x = valid_cycle(lax.axis_index("gx"), lax.axis_size("gx"), vapor_state.shape[1])
    inside_y = valid_cycle(lax.axis_index("gy"), lax.axis_size("gy"), vapor_state.shape[2])
    inside_z = valid_cycle(lax.axis_index("gz"), lax.axis_size("gz"), vapor_state.shape[3])
    inside = inside_x[:, None, None] * inside_y[None, :, None] * inside_z[None, None, :]
    first_section = first_section * inside[None]
    return 0.5 * (
        vapor_state + first_section[:, 1:-1, 1:-1, 1:-1] + GAS_STEP * gas_rate(first_section)
    )


def shards(
    plume_flow_variables, thermal_field, matter_condition, pool_boundary_level, beam_focus_path
):
    cells_x = plume_flow_variables.shape[1]
    cells_z = plume_flow_variables.shape[3]
    height_index = lax.axis_index("gz")
    layers = lax.axis_size("gz")
    heights = height_index * cells_z + jnp.arange(cells_z, dtype=jnp.int32)
    surface_mask = (heights[None, None, :] == pool_boundary_level[:, :, None]).astype(jnp.float32)
    conduct = conductivity(matter_condition)
    workpiece_thermal_mesh = thermal_field
    depth_rim = ((1, 1), (0, 0), (0, 0))
    padded_cond = jnp.pad(extended(conduct, ((("gx", "gz"), 1), ("gy", 2)), 1), depth_rim)
    depth_start = jnp.int32(0)
    x_start = (lax.axis_index("gx") * layers + height_index) * workpiece_thermal_mesh.shape[1]
    on_top = jnp.float32(1.0)
    y_start = lax.axis_index("gy") * workpiece_thermal_mesh.shape[2]
    x_cells = global_cells(x_start, workpiece_thermal_mesh.shape[1])
    y_cells = global_cells(y_start, workpiece_thermal_mesh.shape[2])
    depth_cells = global_cells(depth_start, workpiece_thermal_mesh.shape[0])
    vapor_state = plume_flow_variables
    for outer_step in range(STEPS):
        vapor_state = advance(vapor_state)
        pressure = jnp.sum(vapor_state[5] * surface_mask, axis=2)
        shared = broadcast(pressure, "gz", 0)
        part_rows = cells_x // layers
        pressure_rows = lax.dynamic_slice_in_dim(shared, height_index * part_rows, part_rows, 0)
        fine_pressure = refine(pressure_rows)
        for substep in range(SUBSTEPS):
            padded = jnp.pad(
                extended(workpiece_thermal_mesh, ((("gx", "gz"), 1), ("gy", 2)), 1), depth_rim
            )
            target = beam_focus_path[outer_step * SUBSTEPS + substep]
            change = heat_rate(padded, padded_cond) + laser_heat(
                x_cells, y_cells, depth_cells, target
            )
            cooling = on_top * LATENT_HEAT * evaporation(workpiece_thermal_mesh[0], fine_pressure)
            change = change.at[0].add(-cooling)
            workpiece_thermal_mesh = workpiece_thermal_mesh + HEAT_STEP * change
        top_layer = gather_directly(workpiece_thermal_mesh[0], "gz", 0)
        surface_temp = coarsen(top_layer)
        vapor_mass = evaporation(surface_temp, pressure)[:, :, None] * surface_mask
        vapor_state = vapor_state.at[0].add(VAPOR_SOURCE * vapor_mass)
        vapor_state = vapor_state.at[4].add(RECOIL_PUSH * vapor_mass)
        vapor_state = vapor_state.at[5].add(RECOIL_PRESSURE * vapor_mass)
    return (vapor_state, workpiece_thermal_mesh)


def solution(mesh):
    return jax.shard_map(
        shards,
        mesh=mesh,
        in_specs=(
            P(None, "gx", "gy", "gz"),
            P(None, ("gx", "gz"), "gy"),
            P(None, ("gx", "gz"), "gy"),
            P("gx", "gy"),
            P(),
        ),
        out_specs=(P(None, "gx", "gy", "gz"), P(None, ("gx", "gz"), "gy")),
        check_vma=False,
    )
```

profile of v0, /device:TPU:103, one launch (start us, length us, event | category | flops | bytes accessed | tf_op | source)
XLA Modules:
  0.0 241.1 jit_solution(15691750184898886523)
XLA Ops:
  1.4 4.8 %collective-permute-start.11 = (f32[128,1,32]{0,2,1:T(8,128)S(1)}, f32[128,1,32]{0,2,1:T(8,128)S(1)}, u32[]{:S(2)}, u32[]{:S(2)}) collective-permute-start(f32[128,1,32]{0,2,1:T(8,128)S(1)} %get-tuple-element.184), channel_id=1, source_target_pairs={{0,1},{1,32},{32,33},{33,64},{64,65},{65,96},{96,97},{97,128},{128... | collective-permute-start | bytes 49160 | tf_op jit(solution)/shard_map/ppermute | solution.py:52
  16.4 4.2 %collective-permute-start.6 = (f32[128,8,1]{0,2,1:T(1,128)S(1)}, f32[128,8,1]{0,2,1:T(1,128)S(1)}, u32[]{:S(2)}, u32[]{:S(2)}) collective-permute-start(f32[128,8,1]{0,2,1:T(1,128)S(1)} %get-tuple-element.177), channel_id=1, source_target_pairs={{0,2},{2,4},{4,6},{6,8},{8,10},{10,12},{12,14},{14,16},{16,18},{18... | collective-permute-start | bytes 12296 | tf_op jit(solution)/shard_map/ppermute | solution.py:52
  29.8 4.8 %collective-permute-start = (f32[6,2,16,128]{3,2,1,0:T(8,128)S(1)}, f32[6,2,16,128]{3,2,1,0:T(8,128)S(1)}, u32[]{:S(2)}, u32[]{:S(2)}) collective-permute-start(f32[6,2,16,128]{3,2,1,0:T(8,128)S(1)} %get-tuple-element.164), channel_id=1, source_target_pairs={{0,32},{32,64},{64,96},{96,128},{128,160},{160,192},{192,224},{1,3... | collective-permute-start | bytes 294920 | tf_op jit(solution)/shard_map/ppermute | solution.py:38
  36.5 4.4 %collective-permute-start.12 = (f32[128,1,32]{0,2,1:T(8,128)S(1)}, f32[128,1,32]{0,2,1:T(8,128)S(1)}, u32[]{:S(2)}, u32[]{:S(2)}) collective-permute-start(f32[128,1,32]{0,2,1:T(8,128)S(1)} %get-tuple-element.183), channel_id=1, source_target_pairs={{1,0},{32,1},{33,32},{64,33},{65,64},{96,65},{97,96},{128,97},{129... | collective-permute-start | bytes 49160 | tf_op jit(solution)/shard_map/ppermute | solution.py:53
  42.9 4.9 %collective-permute-start.7 = (f32[128,1,32]{0,2,1:T(8,128)S(1)}, f32[128,1,32]{0,2,1:T(8,128)S(1)}, u32[]{:S(2)}, u32[]{:S(2)}) collective-permute-start(f32[128,1,32]{0,2,1:T(8,128)S(1)} %get-tuple-element.179), channel_id=1, source_target_pairs={{0,1},{1,32},{32,33},{33,64},{64,65},{65,96},{96,97},{97,128},{128... | collective-permute-start | bytes 49160 | tf_op jit(solution)/shard_map/ppermute | solution.py:52
  51.1 5.8 %collective-permute-start.2 = (f32[6,12,2,128]{3,1,2,0:T(8,128)S(1)}, f32[6,12,2,128]{3,1,2,0:T(8,128)S(1)}, u32[]{:S(2)}, u32[]{:S(2)}) collective-permute-start(f32[6,12,2,128]{3,1,2,0:T(8,128)S(1)} %copy.446), channel_id=1, source_target_pairs={{0,2},{2,4},{4,6},{6,8},{8,10},{10,12},{12,14},{14,16},{16,18},{18... | collective-permute-start | bytes 221192 | tf_op jit(solution)/shard_map/ppermute | solution.py:38
  57.1 4.3 %copy.419 = f32[6,12,16,128]{2,1,3,0:T(8,128)} copy(f32[6,12,16,128]{3,2,1,0:T(8,128)S(1)} %constant_dynamic-update-slice_fusion) | data formatting | bytes 1179648 | tf_op jit(solution)/shard_map/concatenate | solution.py:40
  61.5 4.2 %copy.420 = f32[6,12,2,128]{2,1,3,0:T(8,128)} copy(f32[6,12,2,128]{3,1,2,0:T(8,128)S(1)} %collective-permute-done.3) | data formatting | bytes 147456 | tf_op jit(solution)/shard_map/ppermute | solution.py:39
  69.8 8.2 %pad_maximum_fusion = f32[6,12,20,128]{2,1,3,0:T(8,128)S(1)} fusion(f32[6,12,2,128]{2,1,3,0:T(8,128)} %copy.420, f32[6,12,16,128]{2,1,3,0:T(8,128)} %copy.419, f32[6,12,2,128]{2,1,3,0:T(8,128)} %copy.418), kind=kLoop, calls=%fused_computation | loop fusion | flops 368640 | bytes 1474560 | tf_op jit(solution)/shard_map/concatenate | solution.py:40
  81.9 5.7 %collective-permute-start.4 = (f32[6,12,20,2]{2,1,3,0:T(8,128)S(1)}, f32[6,12,20,2]{2,1,3,0:T(8,128)S(1)}, u32[]{:S(2)}, u32[]{:S(2)}) collective-permute-start(f32[6,12,20,2]{2,1,3,0:T(8,128)S(1)} %get-tuple-element.145), channel_id=1, source_target_pairs={{0,1},{2,3},{4,5},{6,7},{8,9},{10,11},{12,13},{14,15},{16,17},{18,... | collective-permute-start | bytes 34568 | tf_op jit(solution)/shard_map/ppermute | solution.py:38
  88.6 4.4 %copy.422 = f32[6,12,20,128]{3,2,1,0:T(8,128)S(1)} copy(f32[6,12,20,128]{2,1,3,0:T(8,128)} %copy-done) | data formatting | bytes 1474560 | tf_op jit(solution)/shard_map/concatenate | solution.py:40
  102.3 4.7 %all-gather = f32[16,16]{1,0:T(8,128)S(1)} all-gather(f32[8,16]{1,0:T(8,128)S(1)} %fusion.102), channel_id=2, replica_groups=mesh['gx'=8,'gy'=16,'gz'=2] {'gz'}, dimensions={0}, use_global_device_ids=true | all-gather | bytes 1536 | tf_op jit(solution)/shard_map/all_gather | solution.py:65
  113.3 4.9 %collective-permute-start.15 = (f32[128,1,32]{0,2,1:T(8,128)S(1)}, f32[128,1,32]{0,2,1:T(8,128)S(1)}, u32[]{:S(2)}, u32[]{:S(2)}) collective-permute-start(f32[128,1,32]{0,2,1:T(8,128)S(1)} %get-tuple-element.175), channel_id=1, source_target_pairs={{0,1},{1,32},{32,33},{33,64},{64,65},{65,96},{96,97},{97,128},{128... | collective-permute-start | bytes 49160 | tf_op jit(solution)/shard_map/ppermute | solution.py:52
  120.8 4.4 %collective-permute-done.17 = f32[128,8,1]{0,2,1:T(1,128)S(1)} collective-permute-done((f32[128,8,1]{0,2,1:T(1,128)S(1)}, f32[128,8,1]{0,2,1:T(1,128)S(1)}, u32[]{:S(2)}, u32[]{:S(2)}) %collective-permute-start.17) | collective-permute-done | bytes 4128 | tf_op jit(solution)/shard_map/ppermute | solution.py:53
  138.6 4.6 %collective-permute-start.18 = (f32[6,2,16,128]{3,2,1,0:T(8,128)S(1)}, f32[6,2,16,128]{3,2,1,0:T(8,128)S(1)}, u32[]{:S(2)}, u32[]{:S(2)}) collective-permute-start(f32[6,2,16,128]{3,2,1,0:T(8,128)S(1)} %get-tuple-element.161), channel_id=1, source_target_pairs={{0,32},{32,64},{64,96},{96,128},{128,160},{160,192},{192,224},{1,3... | collective-permute-start | bytes 294920 | tf_op jit(solution)/shard_map/ppermute | solution.py:38
  153.3 5.5 %collective-permute-start.20 = (f32[6,12,2,128]{3,1,2,0:T(8,128)S(1)}, f32[6,12,2,128]{3,1,2,0:T(8,128)S(1)}, u32[]{:S(2)}, u32[]{:S(2)}) collective-permute-start(f32[6,12,2,128]{3,1,2,0:T(8,128)S(1)} %copy.448), channel_id=1, source_target_pairs={{0,2},{2,4},{4,6},{6,8},{8,10},{10,12},{12,14},{14,16},{16,18},{18... | collective-permute-start | bytes 221192 | tf_op jit(solution)/shard_map/ppermute | solution.py:38
  159.0 4.3 %copy.434 = f32[6,12,16,128]{2,1,3,0:T(8,128)} copy(f32[6,12,16,128]{3,2,1,0:T(8,128)S(1)} %pad_maximum_fusion.8) | data formatting | bytes 1179648 | tf_op jit(solution)/shard_map/concatenate | solution.py:40
  171.7 8.1 %pad_maximum_fusion.1 = f32[6,12,20,128]{2,1,3,0:T(8,128)S(1)} fusion(f32[6,12,2,128]{2,1,3,0:T(8,128)} %copy.435, f32[6,12,16,128]{2,1,3,0:T(8,128)} %copy.434, f32[6,12,2,128]{2,1,3,0:T(8,128)} %copy.433), kind=kLoop, calls=%fused_computation.1 | loop fusion | flops 368640 | bytes 1474560 | tf_op jit(solution)/shard_map/concatenate | solution.py:40
  183.8 8.2 %collective-permute-start.22 = (f32[6,12,20,2]{2,1,3,0:T(8,128)S(1)}, f32[6,12,20,2]{2,1,3,0:T(8,128)}, u32[]{:S(2)}, u32[]{:S(2)}) collective-permute-start(f32[6,12,20,2]{2,1,3,0:T(8,128)S(1)} %get-tuple-element.143), channel_id=1, source_target_pairs={{0,1},{2,3},{4,5},{6,7},{8,9},{10,11},{12,13},{14,15},{16,17},{18,... | collective-permute-start | bytes 34568 | tf_op jit(solution)/shard_map/ppermute | solution.py:38
  192.8 4.4 %copy.437 = f32[6,12,20,128]{3,2,1,0:T(8,128)S(1)} copy(f32[6,12,20,128]{2,1,3,0:T(8,128)} %copy-done.1) | data formatting | bytes 1474560 | tf_op jit(solution)/shard_map/concatenate | solution.py:40
  207.2 4.7 %all-gather.1 = f32[16,16]{1,0:T(8,128)S(1)} all-gather(f32[8,16]{1,0:T(8,128)S(1)} %fusion.103), channel_id=3, replica_groups=mesh['gx'=8,'gy'=16,'gz'=2] {'gz'}, dimensions={0}, use_global_device_ids=true | all-gather | bytes 1536 | tf_op jit(solution)/shard_map/all_gather | solution.py:65
  217.8 4.9 %collective-permute-start.29 = (f32[128,1,32]{0,2,1:T(8,128)S(1)}, f32[128,1,32]{0,2,1:T(8,128)S(1)}, u32[]{:S(2)}, u32[]{:S(2)}) collective-permute-start(f32[128,1,32]{0,2,1:T(8,128)S(1)} %get-tuple-element.167), channel_id=1, source_target_pairs={{0,1},{1,32},{32,33},{33,64},{64,65},{65,96},{96,97},{97,128},{128... | collective-permute-start | bytes 49160 | tf_op jit(solution)/shard_map/ppermute | solution.py:52
  224.6 5.1 %collective-permute-done.31 = f32[128,8,1]{0,2,1:T(1,128)S(1)} collective-permute-done((f32[128,8,1]{0,2,1:T(1,128)S(1)}, f32[128,8,1]{0,2,1:T(1,128)S(1)}, u32[]{:S(2)}, u32[]{:S(2)}) %collective-permute-start.31) | collective-permute-done | bytes 4128 | tf_op jit(solution)/shard_map/ppermute | solution.py:53
  230.7 8.4 %all_to_all.10 = f32[2,1,256]{2,1,0:T(1,128)S(1)} all-to-all(f32[2,1,256]{2,1,0:T(1,128)S(1)} %reshape.697), channel_id=1, replica_groups=mesh['gx'=8,'gy'=16,'gz'=2] {'gz'}, dimensions={0} | all-to-all | bytes 4096 | tf_op jit(solution)/shard_map/all_to_all | solution.py:76
  (277 shorter events, 106.0 us)
Async XLA Ops:
  1.4 41.5 %collective-permute-start.11 = (f32[128,1,32]{0,2,1:T(8,128)S(1)}, f32[128,1,32]{0,2,1:T(8,128)S(1)}, u32[]{:S(2)}, u32[]{:S(2)}) collective-permute-start(f32[128,1,32]{0,2,1:T(8,128)S(1)} %get-tuple-element.184), channel_id=1, source_target_pairs={{0,1},{1,32},{32,33},{33,64},{64,65},{65,96},{96,97},{97,128},{128... | collective-permute-start | bytes 49160 | tf_op jit(solution)/shard_map/ppermute | solution.py:52
  7.0 22.8 %collective-permute-start.10 = (f32[128,8,1]{0,2,1:T(1,128)S(1)}, f32[128,8,1]{0,2,1:T(1,128)S(1)}, u32[]{:S(2)}, u32[]{:S(2)}) collective-permute-start(f32[128,8,1]{0,2,1:T(1,128)S(1)} %get-tuple-element.182), channel_id=1, source_target_pairs={{0,2},{2,4},{4,6},{6,8},{8,10},{10,12},{12,14},{14,16},{16,18},{18... | collective-permute-start | bytes 12296 | tf_op jit(solution)/shard_map/ppermute | solution.py:52
  10.1 24.5 %collective-permute-start.13 = (f32[128,8,1]{0,2,1:T(1,128)S(1)}, f32[128,8,1]{0,2,1:T(1,128)S(1)}, u32[]{:S(2)}, u32[]{:S(2)}) collective-permute-start(f32[128,8,1]{0,2,1:T(1,128)S(1)} %get-tuple-element.181), channel_id=1, source_target_pairs={{2,0},{4,2},{6,4},{8,6},{10,8},{12,10},{14,12},{16,14},{18,16},{20... | collective-permute-start | bytes 12296 | tf_op jit(solution)/shard_map/ppermute | solution.py:53
  13.0 23.6 %collective-permute-start.9 = (f32[128,8,1]{0,2,1:T(1,128)S(1)}, f32[128,8,1]{0,2,1:T(1,128)S(1)}, u32[]{:S(2)}, u32[]{:S(2)}) collective-permute-start(f32[128,8,1]{0,2,1:T(1,128)S(1)} %get-tuple-element.178), channel_id=1, source_target_pairs={{2,0},{4,2},{6,4},{8,6},{10,8},{12,10},{14,12},{16,14},{18,16},{20... | collective-permute-start | bytes 12296 | tf_op jit(solution)/shard_map/ppermute | solution.py:53
  16.4 24.5 %collective-permute-start.6 = (f32[128,8,1]{0,2,1:T(1,128)S(1)}, f32[128,8,1]{0,2,1:T(1,128)S(1)}, u32[]{:S(2)}, u32[]{:S(2)}) collective-permute-start(f32[128,8,1]{0,2,1:T(1,128)S(1)} %get-tuple-element.177), channel_id=1, source_target_pairs={{0,2},{2,4},{4,6},{6,8},{8,10},{10,12},{12,14},{14,16},{16,18},{18... | collective-permute-start | bytes 12296 | tf_op jit(solution)/shard_map/ppermute | solution.py:52
  29.8 19.2 %collective-permute-start = (f32[6,2,16,128]{3,2,1,0:T(8,128)S(1)}, f32[6,2,16,128]{3,2,1,0:T(8,128)S(1)}, u32[]{:S(2)}, u32[]{:S(2)}) collective-permute-start(f32[6,2,16,128]{3,2,1,0:T(8,128)S(1)} %get-tuple-element.164), channel_id=1, source_target_pairs={{0,32},{32,64},{64,96},{96,128},{128,160},{160,192},{192,224},{1,3... | collective-permute-start | bytes 294920 | tf_op jit(solution)/shard_map/ppermute | solution.py:38
  34.6 14.5 %collective-permute-start.1 = (f32[6,2,16,128]{3,2,1,0:T(8,128)S(1)}, f32[6,2,16,128]{3,2,1,0:T(8,128)S(1)}, u32[]{:S(2)}, u32[]{:S(2)}) collective-permute-start(f32[6,2,16,128]{3,2,1,0:T(8,128)S(1)} %get-tuple-element.163), channel_id=1, source_target_pairs={{32,0},{64,32},{96,64},{128,96},{160,128},{192,160},{224,192},{33,... | collective-permute-start | bytes 294920 | tf_op jit(solution)/shard_map/ppermute | solution.py:39
  36.5 12.2 %collective-permute-start.12 = (f32[128,1,32]{0,2,1:T(8,128)S(1)}, f32[128,1,32]{0,2,1:T(8,128)S(1)}, u32[]{:S(2)}, u32[]{:S(2)}) collective-permute-start(f32[128,1,32]{0,2,1:T(8,128)S(1)} %get-tuple-element.183), channel_id=1, source_target_pairs={{1,0},{32,1},{33,32},{64,33},{65,64},{96,65},{97,96},{128,97},{129... | collective-permute-start | bytes 49160 | tf_op jit(solution)/shard_map/ppermute | solution.py:53
  41.0 15.9 %collective-permute-start.8 = (f32[128,1,32]{0,2,1:T(8,128)S(1)}, f32[128,1,32]{0,2,1:T(8,128)S(1)}, u32[]{:S(2)}, u32[]{:S(2)}) collective-permute-start(f32[128,1,32]{0,2,1:T(8,128)S(1)} %get-tuple-element.180), channel_id=1, source_target_pairs={{1,0},{32,1},{33,32},{64,33},{65,64},{96,65},{97,96},{128,97},{129... | collective-permute-start | bytes 49160 | tf_op jit(solution)/shard_map/ppermute | solution.py:53
  42.9 14.0 %collective-permute-start.7 = (f32[128,1,32]{0,2,1:T(8,128)S(1)}, f32[128,1,32]{0,2,1:T(8,128)S(1)}, u32[]{:S(2)}, u32[]{:S(2)}) collective-permute-start(f32[128,1,32]{0,2,1:T(8,128)S(1)} %get-tuple-element.179), channel_id=1, source_target_pairs={{0,1},{1,32},{32,33},{33,64},{64,65},{65,96},{96,97},{97,128},{128... | collective-permute-start | bytes 49160 | tf_op jit(solution)/shard_map/ppermute | solution.py:52
  49.1 12.3 %collective-permute-start.3 = (f32[6,12,2,128]{3,1,2,0:T(8,128)S(1)}, f32[6,12,2,128]{3,1,2,0:T(8,128)S(1)}, u32[]{:S(2)}, u32[]{:S(2)}) collective-permute-start(f32[6,12,2,128]{3,1,2,0:T(8,128)S(1)} %copy.447), channel_id=1, source_target_pairs={{2,0},{4,2},{6,4},{8,6},{10,8},{12,10},{14,12},{16,14},{18,16},{20... | collective-permute-start | bytes 221192 | tf_op jit(solution)/shard_map/ppermute | solution.py:39
  51.1 14.6 %collective-permute-start.2 = (f32[6,12,2,128]{3,1,2,0:T(8,128)S(1)}, f32[6,12,2,128]{3,1,2,0:T(8,128)S(1)}, u32[]{:S(2)}, u32[]{:S(2)}) collective-permute-start(f32[6,12,2,128]{3,1,2,0:T(8,128)S(1)} %copy.446), channel_id=1, source_target_pairs={{0,2},{2,4},{4,6},{6,8},{8,10},{10,12},{12,14},{14,16},{16,18},{18... | collective-permute-start | bytes 221192 | tf_op jit(solution)/shard_map/ppermute | solution.py:38
  80.6 12.3 %collective-permute-start.5 = (f32[6,12,20,2]{2,1,3,0:T(8,128)S(1)}, f32[6,12,20,2]{2,1,3,0:T(8,128)S(1)}, u32[]{:S(2)}, u32[]{:S(2)}) collective-permute-start(f32[6,12,20,2]{2,1,3,0:T(8,128)S(1)} %get-tuple-element.146), channel_id=1, source_target_pairs={{1,0},{3,2},{5,4},{7,6},{9,8},{11,10},{13,12},{15,14},{17,16},{19,... | collective-permute-start | bytes 34568 | tf_op jit(solution)/shard_map/ppermute | solution.py:39
  107.7 13.0 %collective-permute-start.14 = (f32[128,8,1]{0,2,1:T(1,128)S(1)}, f32[128,8,1]{0,2,1:T(1,128)S(1)}, u32[]{:S(2)}, u32[]{:S(2)}) collective-permute-start(f32[128,8,1]{0,2,1:T(1,128)S(1)} %get-tuple-element.174), channel_id=1, source_target_pairs={{0,2},{2,4},{4,6},{6,8},{8,10},{10,12},{12,14},{14,16},{16,18},{18... | collective-permute-start | bytes 12296 | tf_op jit(solution)/shard_map/ppermute | solution.py:52
  111.3 13.8 %collective-permute-start.16 = (f32[128,1,32]{0,2,1:T(8,128)S(1)}, f32[128,1,32]{0,2,1:T(8,128)S(1)}, u32[]{:S(2)}, u32[]{:S(2)}) collective-permute-start(f32[128,1,32]{0,2,1:T(8,128)S(1)} %get-tuple-element.176), channel_id=1, source_target_pairs={{1,0},{32,1},{33,32},{64,33},{65,64},{96,65},{97,96},{128,97},{129... | collective-permute-start | bytes 49160 | tf_op jit(solution)/shard_map/ppermute | solution.py:53
  130.5 16.2 %collective-permute-start.24 = (f32[128,8,1]{0,2,1:T(1,128)S(1)}, f32[128,8,1]{0,2,1:T(1,128)S(1)}, u32[]{:S(2)}, u32[]{:S(2)}) collective-permute-start(f32[128,8,1]{0,2,1:T(1,128)S(1)} %get-tuple-element.170), channel_id=1, source_target_pairs={{0,2},{2,4},{4,6},{6,8},{8,10},{10,12},{12,14},{14,16},{16,18},{18... | collective-permute-start | bytes 12296 | tf_op jit(solution)/shard_map/ppermute | solution.py:52
  132.4 17.7 %collective-permute-start.27 = (f32[128,8,1]{0,2,1:T(1,128)S(1)}, f32[128,8,1]{0,2,1:T(1,128)S(1)}, u32[]{:S(2)}, u32[]{:S(2)}) collective-permute-start(f32[128,8,1]{0,2,1:T(1,128)S(1)} %get-tuple-element.169), channel_id=1, source_target_pairs={{2,0},{4,2},{6,4},{8,6},{10,8},{12,10},{14,12},{16,14},{18,16},{20... | collective-permute-start | bytes 12296 | tf_op jit(solution)/shard_map/ppermute | solution.py:53
  136.7 13.5 %collective-permute-start.19 = (f32[6,2,16,128]{3,2,1,0:T(8,128)S(1)}, f32[6,2,16,128]{3,2,1,0:T(8,128)S(1)}, u32[]{:S(2)}, u32[]{:S(2)}) collective-permute-start(f32[6,2,16,128]{3,2,1,0:T(8,128)S(1)} %get-tuple-element.162), channel_id=1, source_target_pairs={{32,0},{64,32},{96,64},{128,96},{160,128},{192,160},{224,192},{33,... | collective-permute-start | bytes 294920 | tf_op jit(solution)/shard_map/ppermute | solution.py:39
  143.2 15.6 %collective-permute-start.26 = (f32[128,1,32]{0,2,1:T(8,128)S(1)}, f32[128,1,32]{0,2,1:T(8,128)S(1)}, u32[]{:S(2)}, u32[]{:S(2)}) collective-permute-start(f32[128,1,32]{0,2,1:T(8,128)S(1)} %get-tuple-element.172), channel_id=1, source_target_pairs={{1,0},{32,1},{33,32},{64,33},{65,64},{96,65},{97,96},{128,97},{129... | collective-permute-start | bytes 49160 | tf_op jit(solution)/shard_map/ppermute | solution.py:53
  150.3 13.0 %collective-permute-start.21 = (f32[6,12,2,128]{3,1,2,0:T(8,128)S(1)}, f32[6,12,2,128]{3,1,2,0:T(8,128)S(1)}, u32[]{:S(2)}, u32[]{:S(2)}) collective-permute-start(f32[6,12,2,128]{3,1,2,0:T(8,128)S(1)} %copy.449), channel_id=1, source_target_pairs={{2,0},{4,2},{6,4},{8,6},{10,8},{12,10},{14,12},{16,14},{18,16},{20... | collective-permute-start | bytes 221192 | tf_op jit(solution)/shard_map/ppermute | solution.py:39
  153.3 14.3 %collective-permute-start.20 = (f32[6,12,2,128]{3,1,2,0:T(8,128)S(1)}, f32[6,12,2,128]{3,1,2,0:T(8,128)S(1)}, u32[]{:S(2)}, u32[]{:S(2)}) collective-permute-start(f32[6,12,2,128]{3,1,2,0:T(8,128)S(1)} %copy.448), channel_id=1, source_target_pairs={{0,2},{2,4},{4,6},{6,8},{8,10},{10,12},{12,14},{14,16},{16,18},{18... | collective-permute-start | bytes 221192 | tf_op jit(solution)/shard_map/ppermute | solution.py:38
  182.5 14.7 %collective-permute-start.23 = (f32[6,12,20,2]{2,1,3,0:T(8,128)S(1)}, f32[6,12,20,2]{2,1,3,0:T(8,128)S(1)}, u32[]{:S(2)}, u32[]{:S(2)}) collective-permute-start(f32[6,12,20,2]{2,1,3,0:T(8,128)S(1)} %get-tuple-element.144), channel_id=1, source_target_pairs={{1,0},{3,2},{5,4},{7,6},{9,8},{11,10},{13,12},{15,14},{17,16},{19,... | collective-permute-start | bytes 34568 | tf_op jit(solution)/shard_map/ppermute | solution.py:39
  183.8 14.0 %collective-permute-start.22 = (f32[6,12,20,2]{2,1,3,0:T(8,128)S(1)}, f32[6,12,20,2]{2,1,3,0:T(8,128)}, u32[]{:S(2)}, u32[]{:S(2)}) collective-permute-start(f32[6,12,20,2]{2,1,3,0:T(8,128)S(1)} %get-tuple-element.143), channel_id=1, source_target_pairs={{0,1},{2,3},{4,5},{6,7},{8,9},{10,11},{12,13},{14,15},{16,17},{18,... | collective-permute-start | bytes 34568 | tf_op jit(solution)/shard_map/ppermute | solution.py:38
  215.8 13.8 %collective-permute-start.30 = (f32[128,1,32]{0,2,1:T(8,128)S(1)}, f32[128,1,32]{0,2,1:T(8,128)S(1)}, u32[]{:S(2)}, u32[]{:S(2)}) collective-permute-start(f32[128,1,32]{0,2,1:T(8,128)S(1)} %get-tuple-element.168), channel_id=1, source_target_pairs={{1,0},{32,1},{33,32},{64,33},{65,64},{96,65},{97,96},{128,97},{129... | collective-permute-start | bytes 49160 | tf_op jit(solution)/shard_map/ppermute | solution.py:53
  (45 other events, 732.1 us)
where the time goes:
time: 243 us; the launch traced here: 241 us
  starting transfers between devices  114 us (47%)
  local copies, waits for them, and re-layouts  53.2 us (22%)
  other arithmetic  39.5 us (16%)
  blocking collectives  17.8 us (7%)
  waiting for transfers between devices  9.58 us (4%)
  between operations  7.5 us (3%)
    ppermute x10, starting transfers between devices, extended(): lax.ppermute(last, axis, up)  38.9 us
    ppermute x6, starting transfers between devices, padded_2(): before = lax.ppermute(last, axis, up)  34.4 us
    ppermute x10, starting transfers between devices, extended(): lax.ppermute(leading, axis, [(b, a) for a, b in up])  25.2 us
    concatenate x5, other arithmetic, padded_2(): value = jnp.concatenate([before, value, after], axis=dim)  17.9 us
    concatenate x5, local copies, waits for them, and re-layouts, padded_2(): value = jnp.concatenate([before, value, after], axis=dim)  17.4 us
    ppermute x6, starting transfers between devices, padded_2(): after = lax.ppermute(leading, axis, down)  11.3 us
    ppermute x4, local copies, waits for them, and re-layouts, padded_2(): before = lax.ppermute(last, axis, up)  10.3 us
    ppermute x10, waiting for transfers between devices, extended(): lax.ppermute(leading, axis, [(b, a) for a, b in up])  9.52 us
  transfers between devices with their start and end apart: 33, of which 2 were waited for; matrix products, arithmetic and copies ran while one was open for 16% of the time, Pallas kernels for 0%

commit v1 on v0

v1 whole, which is shorter than its diff:
```python
import functools
import math

import jax
import jax.numpy as jnp
from jax import lax
from jax.experimental import pallas as pl
from jax.experimental.pallas import tpu as pltpu
from jax.sharding import PartitionSpec as P

MESH = pl.DeviceIdType.MESH
HI = lax.Precision.HIGHEST
F32 = jnp.float32

NU = (0.2, 0.1, 0.15, 0.15, 0.15, 0.2)
BASE = tuple(1.0 - 1.8 * n for n in NU)
SIDE = tuple(0.3 * n for n in NU)
UPC = tuple(0.3 * n - 0.075 for n in NU)
DNC = tuple(0.3 * n + 0.075 for n in NU)
LASER_POWER = 3.0
LATENT_HEAT = 0.3


def softplus(x):
    return jnp.maximum(x, 0.0) + jnp.log1p(jnp.exp(-jnp.abs(x)))


def nt(a, b, precision=HI):
    return lax.dot_general(
        a, b, (((1,), (1,)), ((), ())), precision=precision, preferred_element_type=F32
    )


def nn(a, b):
    return lax.dot_general(
        a, b, (((1,), (0,)), ((), ())), precision=HI, preferred_element_type=F32
    )


def iota(shape, dim):
    return lax.broadcasted_iota(jnp.int32, shape, dim)


def forward_euler(load, edge):
    def vertical(c):
        center, other = load(c, 0, 0), edge(c)
        lane = iota(center.shape, 1)
        up = pltpu.roll(jnp.where(lane == 0, other, center), 127, 1)
        down = pltpu.roll(jnp.where(lane == 127, other, center), 1, 1)
        return up, down

    u_e, u_w = load(2, 1, 0), load(2, -1, 0)
    v_n, v_s = load(3, 0, 1), load(3, 0, -1)
    w_up, w_dn = vertical(4)
    spread = (u_e - u_w) + (v_n - v_s) + (w_up - w_dn)
    p_e, p_w, p_n, p_s = load(5, 1, 0), load(5, -1, 0), load(5, 0, 1), load(5, 0, -1)
    p_up, p_dn = vertical(5)
    coupled = (
        -0.045 * spread,
        -0.105 * spread,
        -0.15 * (p_e - p_w),
        -0.15 * (p_n - p_s),
        -0.15 * (p_up - p_dn),
        -0.15 * spread,
    )
    out = []
    for c in range(6):
        if c == 4:
            up, dn = w_up, w_dn
        elif c == 5:
            up, dn = p_up, p_dn
        else:
            up, dn = vertical(c)
        sides = (load(c, 1, 0) + load(c, -1, 0)) + (load(c, 0, 1) + load(c, 0, -1))
        out.append(
            BASE[c] * load(c, 0, 0) + SIDE[c] * sides + UPC[c] * up + DNC[c] * dn + coupled[c]
        )
    return out


def kernel(
    sizes,
    u_hbm, t_hbm, m_hbm, lvl_ref, path_ref,
    uo_ref, to_ref,
    A, B, F, UE, FE, ZS, ZR, SS, SR, PS, PR,
    TA, MA, TB, TC, KB, GX, GY, GD, LXB, LYD,
    SA, SB, SK, SGX, SGY, SGD, SGB, SL, SM, LO, LL, MM,
    in_sem, us_sem, ur_sem, zs_sem, zr_sem, ss_sem, sr_sem, ps_sem, pr_sem,
    bs_sem, br_sem,
):
    nx, ny = sizes
    gx, gy, gz = lax.axis_index("gx"), lax.axis_index("gy"), lax.axis_index("gz")
    other = 1 - gz

    def dev(dx, dy, z):
        return (lax.rem(gx + dx + nx, nx), lax.rem(gy + dy + ny, ny), z)

    loads = [
        pltpu.make_async_copy(u_hbm, A.at[:, 2:10, 8:24], in_sem.at[0]),
        pltpu.make_async_copy(t_hbm, TA.at[2:10, 8:40], in_sem.at[1]),
        pltpu.make_async_copy(m_hbm, MA.at[2:10, 8:40], in_sem.at[2]),
    ]
    for copy in loads:
        copy.start()

    barrier = pltpu.get_barrier_semaphore()
    for dx in (-1, 0, 1):
        for dy in (-1, 0, 1):
            for z in (gz, other):
                if dx == 0 and dy == 0 and z is gz:
                    continue
                pl.semaphore_signal(
                    barrier, inc=1, device_id=dev(dx, dy, z), device_id_type=MESH
                )

    sent = []

    def send(src, dst, s_sem, r_sem, target):
        copy = pltpu.make_async_remote_copy(
            src_ref=src, dst_ref=dst, send_sem=s_sem, recv_sem=r_sem,
            device_id=target, device_id_type=MESH,
        )
        copy.start()
        sent.append(copy)

    def arrive(dst, s_sem, r_sem):
        pltpu.make_async_remote_copy(
            src_ref=dst, dst_ref=dst, send_sem=s_sem, recv_sem=r_sem,
            device_id=dev(1, 0, gz), device_id_type=MESH,
        ).wait_recv()

    def vapor_slots(X):
        slots = [X.at[:, 0:2, 8:24], X.at[:, 10:12, 8:24], X.at[:, 2:10, 0:8], X.at[:, 2:10, 24:32]]
        for xi in (1, 10):
            for row in (0, 24):
                slots.append(X.at[:, xi:xi + 1, row:row + 8])
        return slots

    def vapor_sources(own):
        sources = [own(6, 2, 0, 16), own(0, 2, 0, 16), own(0, 8, 8, 8), own(0, 8, 0, 8)]
        for x in (7, 0):
            for y in (8, 0):
                sources.append(own(x, 1, y, 8))
        return sources

    vapor_targets = [(1, 0), (-1, 0), (0, 1), (0, -1), (1, 1), (1, -1), (-1, 1), (-1, -1)]

    def send_vapor(step, own, X):
        slots, sources = vapor_slots(X), vapor_sources(own)
        for n in (0, 1, 4, 5, 6, 7, 2, 3):
            send(sources[n], slots[n], us_sem.at[step, n], ur_sem.at[step, n],
                 dev(*vapor_targets[n], gz))

    def await_vapor(step, X):
        slots = vapor_slots(X)
        for n in range(8):
            arrive(slots[n], us_sem.at[step, n], ur_sem.at[step, n])

    lane8 = iota((8, 128), 1)
    sub8 = iota((8, 128), 0)

    def pack_z(step, X):
        shift = jnp.where(gz == 0, 2, 0)
        turned = lax.rem(lane8 + shift, 128) // 2
        for half in range(2):
            acc = jnp.zeros((8, 128), F32)
            for k in range(64 if half == 0 else 32):
                n = half * 64 + k
                c, x, yt = n // 16, (n // 2) % 8, n % 2
                v = X[c, x + 2, 8 + 8 * yt:16 + 8 * yt, :]
                if k:
                    v = pltpu.roll(v, 2 * k, 1)
                acc = jnp.where(turned == k, v, acc)
            ZS[step, half] = acc

    z_targets = [(0, 0), (1, 0), (-1, 0), (0, 1), (0, -1)]

    def send_z(step):
        for n in range(5):
            send(ZS.at[step], ZR.at[step, n], zs_sem.at[step, n], zr_sem.at[step, n],
                 dev(*z_targets[n], other))

    def await_z(step):
        for n in range(5):
            arrive(ZR.at[step, n], zs_sem.at[step, n], zr_sem.at[step, n])

    edge_keep = lax.rem(lane8 + 2 * gz, 128) < 2

    def flag(cond):
        return jnp.where(cond, 1.0, 0.0)

    def rim_flags():
        return jnp.where(sub8 < 4, flag(gy < ny - 1), flag(gy > 0)) > 0.5

    def unpack_z(step):
        def tile(slot, c, x, yt):
            n = c * 16 + x * 2 + yt
            v = ZR[step, slot, n // 64]
            k = 2 * (n % 64)
            if k:
                v = pltpu.roll(v, 128 - k, 1)
            return jnp.where(edge_keep, v, 0.0)

        for c in range(6):
            for yt in range(2):
                rows = slice(8 + 8 * yt, 16 + 8 * yt)
                for x in range(8):
                    UE[c, x + 1, rows, :] = tile(0, c, x, yt)
                UE[c, 0, rows, :] = tile(1, c, 7, yt)
                UE[c, 9, rows, :] = tile(2, c, 0, yt)
            for x in range(8):
                low, high = tile(3, c, x, 1), tile(4, c, x, 0)
                rim = jnp.where(sub8 < 4, high, low)
                UE[c, x + 1, 0:8, :] = rim
                UE[c, x + 1, 24:32, :] = rim

    def clear_outside(X):
        @pl.when(gx == 0)
        def _():
            X[:, 0:2] = jnp.zeros((6, 2, 32, 128), F32)
            UE[:, 0:1] = jnp.zeros((6, 1, 32, 128), F32)

        @pl.when(gx == nx - 1)
        def _():
            X[:, 10:12] = jnp.zeros((6, 2, 32, 128), F32)
            UE[:, 9:10] = jnp.zeros((6, 1, 32, 128), F32)

        rim_valid = rim_flags()

        @pl.loop(0, 60)
        def _(n):
            c, xi = n // 10, 1 + lax.rem(n, 10)
            rim = jnp.where(sub8 < 4, X[c, xi, 24:32, :], X[c, xi, 0:8, :])
            rim = jnp.where(rim_valid, rim, 0.0)
            X[c, xi, 0:8, :] = rim
            X[c, xi, 24:32, :] = rim

        @pl.when((gy == 0) | (gy == ny - 1))
        def _():
            @pl.loop(0, 60)
            def _(n):
                c, xi = n // 10, lax.rem(n, 10)
                rim = jnp.where(rim_valid, UE[c, xi, 0:8, :], 0.0)
                UE[c, xi, 0:8, :] = rim
                UE[c, xi, 24:32, :] = rim

    def advance(X, emit):
        rim_rows = rim_flags()
        lane16 = iota((16, 128), 1)
        edge_lane = jnp.where(gz == 0, 0, 127)

        @pl.loop(0, 10)
        def _(i):
            xi = i + 1

            def load(c, dx, dy):
                return X[c, xi + dx, 8 + dy:24 + dy, :]

            new = forward_euler(load, lambda c: UE[c, i, 8:24, :])
            for c in range(6):
                F[c, i, 8:24, :] = new[c]

        @pl.loop(0, 8)
        def _(x):
            def load_rim(c, dx, dy):
                start = {0: 0, 1: 1, -1: 23}[dy]
                return X[c, x + 2 + dx, start:start + 8, :]

            new = forward_euler(load_rim, lambda c: UE[c, x + 1, 0:8, :])
            for c in range(6):
                rim = jnp.where(rim_rows, new[c], 0.0)
                F[c, x + 1, 0:8, :] = rim
                F[c, x + 1, 24:32, :] = rim

            def load_edge(c, dx, dy):
                return UE[c, x + 1 + dx, 8 + dy:24 + dy, :]

            new = forward_euler(load_edge, lambda c: X[c, x + 2, 8:24, :])
            for c in range(6):
                FE[c, x] = jnp.where(lane16 == edge_lane, new[c], 0.0)

        @pl.when(gx == 0)
        def _():
            F[:, 0:1] = jnp.zeros((6, 1, 32, 128), F32)

        @pl.when(gx == nx - 1)
        def _():
            F[:, 9:10] = jnp.zeros((6, 1, 32, 128), F32)

        @pl.loop(0, 8)
        def _(x):
            def load(c, dx, dy):
                return F[c, x + 1 + dx, 8 + dy:24 + dy, :]

            new = forward_euler(load, lambda c: FE[c, x])
            for c in range(6):
                emit(c, x, 0.5 * (X[c, x + 2, 8:24, :] + new[c]))

    row_first = gx * 16 - 8
    col_first = gy * 32 - 32
    rows_all, cols_all = nx * 16, ny * 32

    def gauss(cells, centre):
        d = (cells.astype(F32) - centre.astype(F32)) / 6.0
        return jnp.exp(-(d * d))

    def prepare():
        col = col_first + lane8
        col_in = (col >= 0) & (col < cols_all) & (lane8 < 96)
        depth = jnp.exp(-(sub8.astype(F32)) / 4.0)
        for sub in range(4):
            a, b = path_ref[sub, 0], path_ref[sub, 1]
            profile = LASER_POWER * depth * gauss(col, b)

            @pl.loop(0, 32)
            def _(r):
                along = gauss(jnp.full((8, 128), row_first + r, jnp.int32), a)
                SL[sub, pl.ds(pl.multiple_of(r * 8, 8), 8), :] = profile * along

            c48 = gy * 32 - 8 + iota((48, 128), 0)
            d48 = jnp.exp(-(iota((48, 128), 1).astype(F32)) / 4.0)
            LYD[sub] = LASER_POWER * d48 * gauss(c48, b)
            for r in range(12):
                cell = jnp.full((8, 128), (gx * 2 + gz) * 8 - 2 + r, jnp.int32)
                LXB[sub * 12 + r] = gauss(cell, a)

        @pl.loop(0, 32)
        def _(r):
            row = row_first + r
            row_in = flag((row >= 0) & (row < rows_all))
            SM[pl.ds(pl.multiple_of(r * 8, 8), 8), :] = jnp.where(col_in, row_in, 0.0)

        level = jnp.concatenate(
            [lvl_ref[...].astype(F32), jnp.zeros((8, 112), F32)], axis=1)
        SS[4] = level
        eye = jnp.where(iota((16, 128), 0) == iota((16, 128), 1), 1.0, 0.0)
        LO[...] = nt(eye, jnp.concatenate([level, jnp.zeros((120, 128), F32)], axis=0))

    def pack_surface():
        pick = jnp.where(sub8 == lane8, 1.0, 0.0)
        for half in range(2):
            t = TA[2 + 4 * half:6 + 4 * half, 8:40, :].reshape(128, 128)
            m = MA[2 + 4 * half:6 + 4 * half, 8:40, :].reshape(128, 128).astype(F32)
            SS[half] = nt(pick, t)
            SS[2 + half] = nt(pick, m)

    own_slot = (1 + gz) * 3 + 1

    def send_surface():
        for near in (True, False):
            tx = 0 if near else 2 * gz - 1
            block = 1 + gz if near else 3 - 3 * gz
            for ty in (-1, 0, 1):
                for z in (gz, other):
                    if near and ty == 0 and z is gz:
                        continue
                    slot = block * 3 + 1 - ty
                    same = 1 if z is gz else 0
                    n = (6 if near else 0) + (ty + 1) * 2 + same
                    send(SS, SR.at[slot], ss_sem.at[n], sr_sem.at[slot], dev(tx, ty, z))

    def await_surface():
        for slot in range(12):
            if slot in (4, 7):
                @pl.when(own_slot != slot)
                def _():
                    arrive(SR.at[slot], ss_sem.at[0], sr_sem.at[slot])
            else:
                arrive(SR.at[slot], ss_sem.at[0], sr_sem.at[slot])

    def assemble_surface():
        SK[0:8, :] = jnp.zeros((8, 128), F32)
        SK[264:272, :] = jnp.zeros((8, 128), F32)
        SA[0:8, :] = jnp.zeros((8, 128), F32)
        SA[264:272, :] = jnp.zeros((8, 128), F32)
        SB[0:8, :] = jnp.zeros((8, 128), F32)
        SB[264:272, :] = jnp.zeros((8, 128), F32)
        SGX[0:8, :] = jnp.zeros((8, 128), F32)

        def merged(rb, x, first):
            parts = []
            for cb in range(3):
                v = SR[rb * 3 + cb, first + x // 4]
                shift = (32 * cb - 32 * (x % 4)) % 128
                parts.append(pltpu.roll(v, shift, 1) if shift else v)
            return jnp.where(lane8 < 32, parts[0], jnp.where(lane8 < 64, parts[1], parts[2]))

        @pl.loop(0, 4)
        def _(rb):
            for x in range(8):
                at = pl.multiple_of(rb * 64 + x * 8, 8)
                mask = SM[pl.ds(at, 8), :] > 0.5
                phase = merged(rb, x, 2)
                k = jnp.where(phase < 0.5, 0.04, jnp.where(phase < 1.5, 0.15, 0.09))
                SK[pl.ds(at + 8, 8), :] = jnp.where(mask, k, 0.0)
                SA[pl.ds(at + 8, 8), :] = jnp.where(mask, merged(rb, x, 0), 0.0)

        @pl.loop(0, 32)
        def _(r):
            at = pl.multiple_of(r * 8, 8)
            k = SK[pl.ds(at + 8, 8), :]
            SGX[pl.ds(at + 8, 8), :] = 0.5 * (k + SK[pl.ds(at + 16, 8), :])
            SGY[pl.ds(at, 8), :] = 0.5 * (k + pltpu.roll(k, 127, 1))
            SGD[pl.ds(at, 8), :] = jnp.where(sub8 == 7, 0.0, 0.5 * (k + pltpu.roll(k, 7, 0)))
            SGB[pl.ds(at, 8), :] = jnp.where(sub8 == 0, 0.5 * k, 0.0)

        blocks = []
        for rb in (0, 1, 3):
            acc = SR[rb * 3, 4]
            for cb in (1, 2):
                acc = acc + pltpu.roll(SR[rb * 3 + cb, 4], 16 * cb, 1)
            blocks.append(acc)
        blocks.append(jnp.zeros((104, 128), F32))
        eye = jnp.where(iota((48, 128), 0) == iota((48, 128), 1), 1.0, 0.0)
        LL[...] = nt(eye, jnp.concatenate(blocks, axis=0))

    def surface_substep(sub, src, dst, fine_pressure):
        for chunk in range(4):
            base = chunk * 64
            t = src[base + 8:base + 72, :]
            g = SGX[base + 8:base + 72, :]
            change = g * (src[base + 16:base + 80, :] - t) - SGX[base:base + 64, :] * (
                t - src[base:base + 64, :])
            flow = SGY[base:base + 64, :] * (pltpu.roll(t, 127, 1) - t)
            change = change + (flow - pltpu.roll(flow, 1, 1))
            t3 = t.reshape(8, 8, 128)
            gd = SGD[base:base + 64, :].reshape(8, 8, 128)
            flow3 = gd * (pltpu.roll(t3, 7, 1) - t3)
            change = change + (flow3 - pltpu.roll(flow3, 1, 1)).reshape(64, 128)
            change = change - SGB[base:base + 64, :] * t + SL[sub, base:base + 64, :]
            dst[base + 8:base + 72, :] = (t + change) * SM[base:base + 64, :]
        top = src[pl.ds(8, 32, stride=8), :]
        cooling = LATENT_HEAT * softplus(top - 1.0 - 0.5 * fine_pressure)
        cooling = cooling * SM[pl.ds(0, 32, stride=8), :]
        dst[pl.ds(8, 32, stride=8), :] = dst[pl.ds(8, 32, stride=8), :] - cooling

    def pressures(step, X, at_x, at_y):
        lane16 = iota((16, 128), 1)
        height = (lane16 + gz * 128).astype(F32)
        acc = jnp.zeros((16, 128), F32)
        for x in range(8):
            v = X[5, x + at_x, at_y:at_y + 16, :]
            hit = height == LO[:, x:x + 1]
            s = jnp.sum(jnp.where(hit, v, 0.0), axis=1, keepdims=True)
            acc = jnp.where(lane16 == x, s, acc)
        PS[step] = acc

        @pl.when(gz == 0)
        def _():
            PR[step, 4] = acc

    p_targets = [(tx, ty, s) for tx in (-1, 0, 1) for ty in (-1, 0, 1) for s in (0, 1)
                 if (tx, ty, s) != (0, 0, 1)]

    def p_copy(step, n):
        tx, ty, s = p_targets[n]
        slot = (1 - tx) * 3 + 1 - ty
        return pltpu.make_async_remote_copy(
            src_ref=PS.at[step], dst_ref=PR.at[step, slot], send_sem=ps_sem.at[step, n],
            recv_sem=pr_sem.at[step, slot], device_id=dev(tx, ty, gz if s else other),
            device_id_type=MESH)

    def send_pressures(step):
        @pl.when(gz == 0)
        def _():
            for n in range(17):
                p_copy(step, n).start()

    def await_pressures(step):
        for slot in range(9):
            if slot == 4:
                @pl.when(gz == 1)
                def _():
                    arrive(PR.at[step, slot], ps_sem.at[step, 0], pr_sem.at[step, slot])
            else:
                arrive(PR.at[step, slot], ps_sem.at[step, 0], pr_sem.at[step, slot])

    def coarse_pressure(step):
        blocks = []
        for by in range(3):
            acc = PR[step, by]
            for bx in (1, 2):
                acc = acc + pltpu.roll(PR[step, bx * 3 + by], 8 * bx, 1)
            blocks.append(acc)
        return jnp.concatenate(blocks, axis=0)

    def fine_from_coarse(coarse):
        rows = jnp.where(iota((32, 128), 1) == (iota((32, 128), 0) + 8) // 2, 1.0, 0.0)
        cols = jnp.where(iota((128, 128), 0) == iota((128, 128), 1) // 2, 1.0, 0.0)
        padded = jnp.concatenate([coarse, jnp.zeros((80, 128), F32)], axis=0)
        return nn(nt(rows, padded), cols)

    def mass_from_surface(ref, coarse):
        top = jnp.concatenate(
            [ref[pl.ds(8, 32, stride=8), :], jnp.zeros((96, 128), F32)], axis=0)
        cols = jnp.where(iota((48, 128), 0) == iota((48, 128), 1) // 2, 0.25, 0.0)
        i = iota((128, 128), 0)
        rows = jnp.where((iota((128, 128), 1) == (i + 8) // 2) & (i < 32), 1.0, 0.0)
        surface = nn(nt(cols, top), rows)
        mass = softplus(surface - 1.0 - 0.5 * coarse)
        y = gy * 16 - 16 + iota((48, 128), 0)
        x = gx * 8 - 8 + iota((48, 128), 1)
        inside = (y >= 0) & (y < ny * 16) & (x >= 0) & (x < nx * 8)
        return jnp.where(inside, mass, 0.0)

    def with_rim(v):
        rim = jnp.where(sub8 < 4, v[32:40], v[8:16])
        return jnp.concatenate([rim, v[16:32], rim], axis=0)

    row_block = gx * 2 + gz
    dn_row, up_row = -(1 - gz), gz

    def bulk_slots(X):
        slots = [X.at[0:2, 8:40], X.at[10:12, 8:40], X.at[2:10, 0:8], X.at[2:10, 40:48]]
        for r in (1, 10):
            for c in (0, 40):
                slots.append(X.at[r:r + 1, c:c + 8])
        return slots

    def bulk_sources(X, r0, c0):
        def own(r, nr, c, nc):
            return X.at[r0 + r:r0 + r + nr, c0 + c:c0 + c + nc]

        sources = [own(6, 2, 0, 32), own(0, 2, 0, 32), own(0, 8, 24, 8), own(0, 8, 0, 8)]
        for r in (7, 0):
            for c in (24, 0):
                sources.append(own(r, 1, c, 8))
        return sources

    def send_bulk(kind, X, r0, c0, D):
        targets = [dev(up_row, 0, other), dev(dn_row, 0, other), dev(0, 1, gz), dev(0, -1, gz)]
        for tx in (up_row, dn_row):
            for ty in (1, -1):
                targets.append(dev(tx, ty, other))
        sources, slots = bulk_sources(X, r0, c0), bulk_slots(D)
        for n in range(8):
            send(sources[n], slots[n], bs_sem.at[kind, n], br_sem.at[kind, n], targets[n])

    def await_bulk(kind, D):
        slots = bulk_slots(D)
        for n in range(8):
            arrive(slots[n], bs_sem.at[kind, n], br_sem.at[kind, n])

    def clear_bulk(X):
        @pl.when(row_block == 0)
        def _():
            X[0:2] = jnp.zeros((2, 48, 128), F32)

        @pl.when(row_block == 2 * nx - 1)
        def _():
            X[10:12] = jnp.zeros((2, 48, 128), F32)

        @pl.when(gy == 0)
        def _():
            X[:, 0:8] = jnp.zeros((12, 8, 128), F32)

        @pl.when(gy == ny - 1)
        def _():
            X[:, 40:48] = jnp.zeros((12, 8, 128), F32)

    def prepare_bulk():
        @pl.loop(0, 12)
        def _(r):
            m = MA[r]
            KB[r] = jnp.where(m == 0, 0.04, jnp.where(m == 1, 0.15, 0.09))

        clear_bulk(KB)

        @pl.loop(0, 11)
        def _(r):
            k = KB[r]
            GX[r] = 0.5 * (k + KB[r + 1])
            GY[r] = 0.5 * (k + pltpu.roll(k, 47, 0))
            last = iota((48, 128), 1) == 127
            GD[r] = 0.5 * (k + jnp.where(last, 0.0, pltpu.roll(k, 127, 1)))

    def bulk_substep(sub, src, dst, low, high, own_only=False):
        col = gy * 32 - 8 + iota((48, 128), 0)
        col_in = jnp.where((col >= 0) & (col < cols_all), 1.0, 0.0)
        last = iota((48, 128), 1) == 127

        @pl.loop(low, high)
        def _(r):
            t = src[r]
            change = GX[r] * (src[r + 1] - t) - GX[r - 1] * (t - src[r - 1])
            flow = GY[r] * (pltpu.roll(t, 47, 0) - t)
            change = change + (flow - pltpu.roll(flow, 1, 0))
            flow = GD[r] * (jnp.where(last, 0.0, pltpu.roll(t, 127, 1)) - t)
            change = change + (flow - pltpu.roll(flow, 1, 1))
            along = LXB[sub * 12 + r]
            laser = LYD[sub] * jnp.concatenate([along] * 6, axis=0)
            row = row_block * 8 - 2 + r
            row_in = jnp.where((row >= 0) & (row < rows_all), 1.0, 0.0)
            new = (t + change + laser) * (col_in * row_in)
            if own_only:
                dst[r, 8:40, :] = new[8:40]
            else:
                dst[r] = new

    prepare()
    loads[0].wait()
    pack_z(0, A)
    loads[1].wait()
    loads[2].wait()
    pack_surface()
    SR[own_slot] = SS[...]
    pl.semaphore_wait(barrier, 17)

    send_vapor(0, lambda x, n, y, m: u_hbm.at[:, x:x + n, y:y + m], A)
    send_z(0)
    send_surface()
    send_bulk(0, t_hbm, 0, 0, TA)
    send_bulk(1, m_hbm, 0, 0, MA)

    await_z(0)
    unpack_z(0)
    await_vapor(0, A)
    clear_outside(A)

    def to_b(c, x, v):
        B[c, x + 2, 8:24, :] = v

    advance(A, to_b)
    first = len(sent)
    send_vapor(1, lambda x, n, y, m: B.at[:, x + 2:x + 2 + n, y + 8:y + 8 + m], B)
    sent_b = sent[first:]
    del sent[first:]
    pressures(0, B, 2, 8)
    send_pressures(0)
    pack_z(1, B)
    send_z(1)

    await_surface()
    assemble_surface()
    await_bulk(0, TA)
    await_bulk(1, MA)
    clear_bulk(TA)
    prepare_bulk()
    bulk_substep(0, TA, TC, 1, 11)
    bulk_substep(1, TC, TB, 2, 10, True)
    send_bulk(2, TB, 2, 8, TB)

    await_pressures(0)
    coarse = coarse_pressure(0)
    fine = fine_from_coarse(coarse)
    surface_substep(0, SA, SB, fine)
    surface_substep(1, SB, SA, fine)
    MM[...] = with_rim(mass_from_surface(SA, coarse))
    LL[0:32, :] = with_rim(LL[...])

    await_z(1)
    unpack_z(1)
    await_vapor(1, B)
    clear_outside(B)
    for copy in sent_b:
        copy.wait_send()
    lane32 = iota((32, 128), 1)
    height = (lane32 + gz * 128).astype(F32)
    height_edge = (lane32 + other * 128).astype(F32)
    for xi in range(12):
        mass = jnp.broadcast_to(MM[:, xi + 6:xi + 7], (32, 128))
        level = jnp.broadcast_to(LL[0:32, xi + 6:xi + 7], (32, 128))
        field = jnp.where(height == level, mass, 0.0)
        B[0, xi] = B[0, xi] + 0.5 * field
        B[4, xi] = B[4, xi] + 0.4 * field
        B[5, xi] = B[5, xi] + 0.6 * field
        if 1 <= xi <= 10:
            @pl.when(gz == 1)
            def _():
                edge = jnp.where((height_edge == level) & (lane32 >= 126), mass, 0.0)
                UE[0, xi - 1] = UE[0, xi - 1] + 0.5 * edge
                UE[4, xi - 1] = UE[4, xi - 1] + 0.4 * edge
                UE[5, xi - 1] = UE[5, xi - 1] + 0.6 * edge

    def to_out(c, x, v):
        uo_ref[c, x] = v

    advance(B, to_out)
    pressures(1, uo_ref, 0, 0)
    send_pressures(1)

    await_bulk(2, TB)
    clear_bulk(TB)
    bulk_substep(2, TB, TC, 1, 11)
    bulk_substep(3, TC, TA, 2, 10, True)

    await_pressures(1)
    coarse = coarse_pressure(1)
    fine = fine_from_coarse(coarse)
    surface_substep(2, SA, SB, fine)
    surface_substep(3, SB, SA, fine)
    mass_now = mass_from_surface(SA, coarse)[16:32]
    lane16 = iota((16, 128), 1)
    height = (lane16 + gz * 128).astype(F32)
    for x in range(8):
        mass = jnp.broadcast_to(mass_now[:, x + 8:x + 9], (16, 128))
        level = jnp.broadcast_to(LO[:, x:x + 1], (16, 128))
        field = jnp.where(height == level, mass, 0.0)
        uo_ref[0, x] = uo_ref[0, x] + 0.5 * field
        uo_ref[4, x] = uo_ref[4, x] + 0.4 * field
        uo_ref[5, x] = uo_ref[5, x] + 0.6 * field

    eye = jnp.where(iota((128, 128), 0) == iota((128, 128), 1), 1.0, 0.0)
    for half in range(2):
        acc = jnp.zeros((8, 128), F32)
        for i in range(4):
            at = pl.multiple_of((9 + gz * 8 + 4 * half + i) * 8, 8)
            v = SA[pl.ds(at, 8), :]
            shift = (32 * i - 32) % 128
            v = pltpu.roll(v, shift, 1) if shift else v
            acc = jnp.where(lane8 // 32 == i, v, acc)
        turned = nt(eye, jnp.concatenate([acc, jnp.zeros((120, 128), F32)], axis=0))
        turned = turned.reshape(4, 32, 128)
        shallow = iota((4, 32, 128), 2) < 4
        deep = TA[2 + 4 * half:6 + 4 * half, 8:40, :]
        to_ref[4 * half:4 * half + 4] = jnp.where(shallow, turned, deep)

    for copy in sent:
        copy.wait_send()

    @pl.when(gz == 0)
    def _():
        for step in range(2):
            for n in range(17):
                p_copy(step, n).wait_send()


def solution(mesh):
    sizes = (mesh.shape["gx"], mesh.shape["gy"])

    def shards(vapor, thermal, phase, level, path):
        anywhere = pl.BlockSpec(memory_space=pl.ANY)
        vmem = pl.BlockSpec(memory_space=pltpu.VMEM)
        dma = pltpu.SemaphoreType.DMA
        row = (12, 48, 128)
        gas, temp = pl.pallas_call(
            functools.partial(kernel, sizes),
            out_shape=(
                jax.ShapeDtypeStruct((6, 8, 16, 128), F32),
                jax.ShapeDtypeStruct((8, 32, 128), F32),
            ),
            in_specs=[anywhere, anywhere, anywhere, vmem, pl.BlockSpec(memory_space=pltpu.SMEM)],
            out_specs=(vmem, vmem),
            scratch_shapes=[
                pltpu.VMEM((6, 12, 32, 128), F32), pltpu.VMEM((6, 12, 32, 128), F32),
                pltpu.VMEM((6, 10, 32, 128), F32), pltpu.VMEM((6, 10, 32, 128), F32),
                pltpu.VMEM((6, 8, 16, 128), F32),
                pltpu.VMEM((2, 2, 8, 128), F32), pltpu.VMEM((2, 5, 2, 8, 128), F32),
                pltpu.VMEM((5, 8, 128), F32), pltpu.VMEM((12, 5, 8, 128), F32),
                pltpu.VMEM((2, 16, 128), F32), pltpu.VMEM((2, 9, 16, 128), F32),
                pltpu.VMEM(row, F32), pltpu.VMEM(row, jnp.int32), pltpu.VMEM(row, F32),
                pltpu.VMEM(row, F32), pltpu.VMEM(row, F32), pltpu.VMEM(row, F32),
                pltpu.VMEM(row, F32), pltpu.VMEM(row, F32),
                pltpu.VMEM((48, 8, 128), F32), pltpu.VMEM((4, 48, 128), F32),
                pltpu.VMEM((272, 128), F32), pltpu.VMEM((272, 128), F32),
                pltpu.VMEM((272, 128), F32), pltpu.VMEM((264, 128), F32),
                pltpu.VMEM((256, 128), F32), pltpu.VMEM((256, 128), F32),
                pltpu.VMEM((256, 128), F32), pltpu.VMEM((4, 256, 128), F32),
                pltpu.VMEM((256, 128), F32), pltpu.VMEM((16, 128), F32),
                pltpu.VMEM((48, 128), F32), pltpu.VMEM((32, 128), F32),
                dma((3,)), dma((2, 8)), dma((2, 8)), dma((2, 5)), dma((2, 5)),
                dma((12,)), dma((12,)), dma((2, 17)), dma((2, 9)),
                dma((3, 8)), dma((3, 8)),
            ],
            compiler_params=pltpu.CompilerParams(collective_id=0, has_side_effects=True),
        )(vapor, jnp.transpose(thermal, (1, 2, 0)), jnp.transpose(phase, (1, 2, 0)), level, path)
        return gas, jnp.transpose(temp, (2, 0, 1))

    return jax.shard_map(
        shards,
        mesh=mesh,
        in_specs=(
            P(None, "gx", "gy", "gz"),
            P(None, ("gx", "gz"), "gy"),
            P(None, ("gx", "gz"), "gy"),
            P("gx", "gy"),
            P(),
        ),
        out_specs=(P(None, "gx", "gy", "gz"), P(None, ("gx", "gz"), "gy")),
        check_vma=False,
    )
```

time: 243 us -> 52.7 us (0.22)
  the two profiles are of different devices: /device:TPU:103 before, /device:TPU:1 now
where the time goes in v1:
time: 52.7 us; the launch traced here: 52.5 us
  Pallas kernels  48.1 us (91%)
  local copies, waits for them, and re-layouts  3.8 us (7%)
  between operations  0.66 us (1%)
    pallas_call x1, Pallas kernels, shards(): pl.pallas_call(functools.partial(kernel, sizes), out_shape=(jax.ShapeDtyp...  48.1 us
    unnamed x7, local copies, waits for them, and re-layouts  3.8 us

profile of v1, /device:TPU:1, one launch (start us, length us, event | category | flops | bytes accessed | tf_op | source)
XLA Modules:
  0.0 52.5 jit_solution(12096094037236369928)
XLA Ops:
  0.6 0.0 copy-start.1
  0.6 0.7 %copy-done.1 = s32[4,2]{0,1:T(2,128)S(1)} copy-done((s32[4,2]{0,1:T(2,128)S(1)}, s32[4,2]{0,1:T(2,128)}, u32[]{:S(2)}) %copy-start.1) | copy-done | bytes 56
  1.3 0.7 %copy.7.path_ref = s32[4,2]{1,0:T(4,128)} copy(s32[4,2]{0,1:T(2,128)S(1)} %copy-done.1) | data formatting | bytes 64 | tf_op args[4]
  2.0 48.1 %shard_map.68 = (f32[6,8,16,128]{3,2,1,0:T(8,128)}, f32[8,32,128]{2,1,0:T(8,128)}) custom-call(f32[6,8,16,128]{3,2,1,0:T(8,128)} %u_hbm.1, f32[8,32,128]{2,1,0:T(8,128)} %bitcast.3, s32[8,32,128]{2,1,0:T(8,128)} %bitcast.4, s32[8,16]{1,0:T(8,128)} %lvl_ref.1, s32[4,2]{1,0:T(4,128)} %copy.7.path_ref), custom_call_target="tpu_custom_call" | custom-call | tf_op jit(solution)/shard_map/pallas_call | solution.py:736
  50.0 0.0 copy-start
  50.0 1.8 %copy.10 = f32[6,8,16,128]{3,2,1,0:T(8,128)} copy(f32[6,8,16,128]{3,2,1,0:T(8,128)} %get-tuple-element.8) | data formatting | bytes 786432
  51.9 0.0 copy-done
  51.9 0.7 %copy.11 = f32[128,8,32]{0,2,1:T(8,128)} copy(f32[128,8,32]{0,2,1:T(8,128)S(1)} %bitcast.5) | data formatting | bytes 262144
Async XLA Ops:
  0.6 0.7 %copy-start.1 = (s32[4,2]{0,1:T(2,128)S(1)}, s32[4,2]{0,1:T(2,128)}, u32[]{:S(2)}) copy-start(s32[4,2]{0,1:T(2,128)} %param.9) | copy-start | bytes 100
  50.0 1.8 %copy-start = (f32[8,32,128]{2,1,0:T(8,128)S(1)}, f32[8,32,128]{2,1,0:T(8,128)}, u32[]{:S(2)}) copy-start(f32[8,32,128]{2,1,0:T(8,128)} %get-tuple-element.5) | copy-start | bytes 393220

commit v2 on v1

--- a/solution.py
+++ b/solution.py
@@ -227,29 +227,29 @@
 
         rim_valid = rim_flags()
 
-        @pl.loop(0, 60)
-        def _(n):
-            c, xi = n // 10, 1 + lax.rem(n, 10)
-            rim = jnp.where(sub8 < 4, X[c, xi, 24:32, :], X[c, xi, 0:8, :])
-            rim = jnp.where(rim_valid, rim, 0.0)
-            X[c, xi, 0:8, :] = rim
-            X[c, xi, 24:32, :] = rim
+        @pl.loop(1, 11, unroll=5)
+        def _(xi):
+            for c in range(6):
+                rim = jnp.where(sub8 < 4, X[c, xi, 24:32, :], X[c, xi, 0:8, :])
+                rim = jnp.where(rim_valid, rim, 0.0)
+                X[c, xi, 0:8, :] = rim
+                X[c, xi, 24:32, :] = rim
 
         @pl.when((gy == 0) | (gy == ny - 1))
         def _():
-            @pl.loop(0, 60)
-            def _(n):
-                c, xi = n // 10, lax.rem(n, 10)
-                rim = jnp.where(rim_valid, UE[c, xi, 0:8, :], 0.0)
-                UE[c, xi, 0:8, :] = rim
-                UE[c, xi, 24:32, :] = rim
+            @pl.loop(0, 10, unroll=2)
+            def _(xi):
+                for c in range(6):
+                    rim = jnp.where(rim_valid, UE[c, xi, 0:8, :], 0.0)
+                    UE[c, xi, 0:8, :] = rim
+                    UE[c, xi, 24:32, :] = rim
 
     def advance(X, emit):
         rim_rows = rim_flags()
         lane16 = iota((16, 128), 1)
         edge_lane = jnp.where(gz == 0, 0, 127)
 
-        @pl.loop(0, 10)
+        @pl.loop(0, 10, unroll=2)
         def _(i):
             xi = i + 1
 
@@ -260,7 +260,7 @@
             for c in range(6):
                 F[c, i, 8:24, :] = new[c]
 
-        @pl.loop(0, 8)
+        @pl.loop(0, 8, unroll=2)
         def _(x):
             def load_rim(c, dx, dy):
                 start = {0: 0, 1: 1, -1: 23}[dy]
@@ -287,7 +287,7 @@
         def _():
             F[:, 9:10] = jnp.zeros((6, 1, 32, 128), F32)
 
-        @pl.loop(0, 8)
+        @pl.loop(0, 8, unroll=2)
         def _(x):
             def load(c, dx, dy):
                 return F[c, x + 1 + dx, 8 + dy:24 + dy, :]
@@ -309,10 +309,10 @@
         col_in = (col >= 0) & (col < cols_all) & (lane8 < 96)
         depth = jnp.exp(-(sub8.astype(F32)) / 4.0)
         for sub in range(4):
-            a, b = path_ref[sub, 0], path_ref[sub, 1]
+            a, b = path_ref[0, sub], path_ref[1, sub]
             profile = LASER_POWER * depth * gauss(col, b)
 
-            @pl.loop(0, 32)
+            @pl.loop(0, 32, unroll=8)
             def _(r):
                 along = gauss(jnp.full((8, 128), row_first + r, jnp.int32), a)
                 SL[sub, pl.ds(pl.multiple_of(r * 8, 8), 8), :] = profile * along
@@ -324,7 +324,7 @@
                 cell = jnp.full((8, 128), (gx * 2 + gz) * 8 - 2 + r, jnp.int32)
                 LXB[sub * 12 + r] = gauss(cell, a)
 
-        @pl.loop(0, 32)
+        @pl.loop(0, 32, unroll=8)
         def _(r):
             row = row_first + r
             row_in = flag((row >= 0) & (row < rows_all))
@@ -395,7 +395,7 @@
                 SK[pl.ds(at + 8, 8), :] = jnp.where(mask, k, 0.0)
                 SA[pl.ds(at + 8, 8), :] = jnp.where(mask, merged(rb, x, 0), 0.0)
 
-        @pl.loop(0, 32)
+        @pl.loop(0, 32, unroll=8)
         def _(r):
             at = pl.multiple_of(r * 8, 8)
             k = SK[pl.ds(at + 8, 8), :]
@@ -559,14 +559,14 @@
             X[:, 40:48] = jnp.zeros((12, 8, 128), F32)
 
     def prepare_bulk():
-        @pl.loop(0, 12)
+        @pl.loop(0, 12, unroll=6)
         def _(r):
             m = MA[r]
             KB[r] = jnp.where(m == 0, 0.04, jnp.where(m == 1, 0.15, 0.09))
 
         clear_bulk(KB)
 
-        @pl.loop(0, 11)
+        @pl.loop(0, 11, unroll=11)
         def _(r):
             k = KB[r]
             GX[r] = 0.5 * (k + KB[r + 1])
@@ -579,7 +579,7 @@
         col_in = jnp.where((col >= 0) & (col < cols_all), 1.0, 0.0)
         last = iota((48, 128), 1) == 127
 
-        @pl.loop(low, high)
+        @pl.loop(low, high, unroll=(high - low) // 2)
         def _(r):
             t = src[r]
             change = GX[r] * (src[r + 1] - t) - GX[r - 1] * (t - src[r - 1])
@@ -597,17 +597,16 @@
             else:
                 dst[r] = new
 
-    prepare()
+    pl.semaphore_wait(barrier, 17)
+    send_vapor(0, lambda x, n, y, m: u_hbm.at[:, x:x + n, y:y + m], A)
     loads[0].wait()
     pack_z(0, A)
+    send_z(0)
+    prepare()
     loads[1].wait()
     loads[2].wait()
     pack_surface()
     SR[own_slot] = SS[...]
-    pl.semaphore_wait(barrier, 17)
-
-    send_vapor(0, lambda x, n, y, m: u_hbm.at[:, x:x + n, y:y + m], A)
-    send_z(0)
     send_surface()
     send_bulk(0, t_hbm, 0, 0, TA)
     send_bulk(1, m_hbm, 0, 0, MA)
@@ -736,8 +735,8 @@
         gas, temp = pl.pallas_call(
             functools.partial(kernel, sizes),
             out_shape=(
-                jax.ShapeDtypeStruct((6, 8, 16, 128), F32),
-                jax.ShapeDtypeStruct((8, 32, 128), F32),
+                pltpu.VMEM((6, 8, 16, 128), F32),
+                pltpu.VMEM((8, 32, 128), F32),
             ),
             in_specs=[anywhere, anywhere, anywhere, vmem, pl.BlockSpec(memory_space=pltpu.SMEM)],
             out_specs=(vmem, vmem),
@@ -763,7 +762,7 @@
                 dma((3, 8)), dma((3, 8)),
             ],
             compiler_params=pltpu.CompilerParams(collective_id=0, has_side_effects=True),
-        )(vapor, jnp.transpose(thermal, (1, 2, 0)), jnp.transpose(phase, (1, 2, 0)), level, path)
+        )(vapor, jnp.transpose(thermal, (1, 2, 0)), jnp.transpose(phase, (1, 2, 0)), level, path.T)
         return gas, jnp.transpose(temp, (2, 0, 1))
 
     return jax.shard_map(

time: 52.7 us -> 45.1 us (0.86)
  Pallas kernels: 48.1 us -> 42.9 us
  local copies, waits for them, and re-layouts: 3.8 us -> 1.4 us
    pallas_call x1, Pallas kernels: 48.1 us -> 42.9 us  [shards(): pl.pallas_call(functools.partial(kernel, sizes), out_shape=(pltpu.VMEM((6...]
    unnamed x7 -> x2, local copies, waits for them, and re-layouts: 3.8 us -> 1.4 us
where the time goes in v2:
time: 45.1 us; the launch traced here: 44.9 us
  Pallas kernels  42.9 us (95%)
  local copies, waits for them, and re-layouts  1.4 us (3%)
  between operations  0.64 us (1%)
    pallas_call x1, Pallas kernels, shards(): pl.pallas_call(functools.partial(kernel, sizes), out_shape=(pltpu.VMEM((6...  42.9 us
    unnamed x2, local copies, waits for them, and re-layouts  1.4 us

profile of v2, /device:TPU:1, one launch (start us, length us, event | category | flops | bytes accessed | tf_op | source)
XLA Modules:
  0.0 44.9 jit_solution(14096632936009841923)
XLA Ops:
  0.6 42.9 %shard_map.68 = (f32[6,8,16,128]{3,2,1,0:T(8,128)S(1)}, f32[8,32,128]{2,1,0:T(8,128)S(1)}) custom-call(f32[6,8,16,128]{3,2,1,0:T(8,128)} %u_hbm.1, f32[8,32,128]{2,1,0:T(8,128)} %bitcast.5, s32[8,32,128]{2,1,0:T(8,128)} %bitcast.6, s32[8,16]{1,0:T(8,128)} %lvl_ref.1, s32[2,4]{1,0:T(2,128)} %bitcast.7), custom_call_target="tpu_custom_call" | custom-call | tf_op jit(solution)/shard_map/pallas_call | solution.py:735
  43.5 0.7 %copy.9 = f32[6,8,16,128]{3,2,1,0:T(8,128)} copy(f32[6,8,16,128]{3,2,1,0:T(8,128)S(1)} %get-tuple-element.6) | data formatting | bytes 786432
  44.3 0.7 %copy.10 = f32[128,8,32]{0,2,1:T(8,128)} copy(f32[128,8,32]{0,2,1:T(8,128)S(1)} %bitcast.4) | data formatting | bytes 262144

commit v3 on v2

--- a/solution.py
+++ b/solution.py
@@ -103,44 +103,71 @@
     for copy in loads:
         copy.start()
 
+    def exists(dx, dy):
+        tests = []
+        for at, d, size in ((gx, dx, nx), (gy, dy, ny)):
+            if not (isinstance(d, int) and d == 0):
+                tests.append((at + d >= 0) & (at + d < size))
+        if not tests:
+            return None
+        return tests[0] if len(tests) == 1 else tests[0] & tests[1]
+
+    def when(cond, body):
+        if cond is None:
+            body()
+        else:
+            pl.when(cond)(body)
+
+    SR[...] = jnp.zeros((12, 5, 8, 128), F32)
+    PR[...] = jnp.zeros((2, 9, 16, 128), F32)
+
     barrier = pltpu.get_barrier_semaphore()
+
+    def greet(dx, dy, z):
+        when(exists(dx, dy), lambda: pl.semaphore_signal(
+            barrier, inc=1, device_id=dev(dx, dy, z), device_id_type=MESH))
+
     for dx in (-1, 0, 1):
         for dy in (-1, 0, 1):
             for z in (gz, other):
-                if dx == 0 and dy == 0 and z is gz:
-                    continue
-                pl.semaphore_signal(
-                    barrier, inc=1, device_id=dev(dx, dy, z), device_id_type=MESH
-                )
+                if not (dx == 0 and dy == 0 and z is gz):
+                    greet(dx, dy, z)
+    beside_x = 3 - jnp.where(gx == 0, 1, 0) - jnp.where(gx == nx - 1, 1, 0)
+    beside_y = 3 - jnp.where(gy == 0, 1, 0) - jnp.where(gy == ny - 1, 1, 0)
 
     sent = []
 
+    def remote(src, dst, s_sem, r_sem, target):
+        return pltpu.make_async_remote_copy(
+            src_ref=src, dst_ref=dst, send_sem=s_sem, recv_sem=r_sem,
+            device_id=dev(*target), device_id_type=MESH,
+        )
+
     def send(src, dst, s_sem, r_sem, target):
-        copy = pltpu.make_async_remote_copy(
-            src_ref=src, dst_ref=dst, send_sem=s_sem, recv_sem=r_sem,
-            device_id=target, device_id_type=MESH,
-        )
-        copy.start()
-        sent.append(copy)
-
-    def arrive(dst, s_sem, r_sem):
-        pltpu.make_async_remote_copy(
-            src_ref=dst, dst_ref=dst, send_sem=s_sem, recv_sem=r_sem,
-            device_id=dev(1, 0, gz), device_id_type=MESH,
-        ).wait_recv()
+        args = (src, dst, s_sem, r_sem, target)
+        cond = exists(target[0], target[1])
+        when(cond, lambda: remote(*args).start())
+        sent.append((cond, args))
+
+    def drain(items):
+        for cond, args in items:
+            when(cond, lambda: remote(*args).wait_send())
+
+    def arrive(dst, s_sem, r_sem, dx, dy):
+        when(exists(dx, dy), lambda: remote(dst, dst, s_sem, r_sem, (1, 0, gz)).wait_recv())
 
     def vapor_slots(X):
-        slots = [X.at[:, 0:2, 8:24], X.at[:, 10:12, 8:24], X.at[:, 2:10, 0:8], X.at[:, 2:10, 24:32]]
+        slots = [X.at[:, 0:2, 8:24], X.at[:, 10:12, 8:24], X.at[:, 2:10, 6:8], X.at[:, 2:10, 24:26]]
         for xi in (1, 10):
-            for row in (0, 24):
-                slots.append(X.at[:, xi:xi + 1, row:row + 8])
+            for row in (7, 24):
+                slots.append(X.at[:, xi:xi + 1, row:row + 1])
         return slots
 
     def vapor_sources(own):
-        sources = [own(6, 2, 0, 16), own(0, 2, 0, 16), own(0, 8, 8, 8), own(0, 8, 0, 8)]
+        sources = [own(6, 2, 0, 16), own(0, 2, 0, 16), own(0, 8, 14, 2), own(0, 8, 0, 2)]
         for x in (7, 0):
-            for y in (8, 0):
-                sources.append(own(x, 1, y, 8))
+            for y in (15, 0):
+                sources.append(own(x, 1, y, 1))
         return sources
 
     vapor_targets = [(1, 0), (-1, 0), (0, 1), (0, -1), (1, 1), (1, -1), (-1, 1), (-1, -1)]
@@ -149,12 +176,13 @@
         slots, sources = vapor_slots(X), vapor_sources(own)
         for n in (0, 1, 4, 5, 6, 7, 2, 3):
             send(sources[n], slots[n], us_sem.at[step, n], ur_sem.at[step, n],
-                 dev(*vapor_targets[n], gz))
+                 (*vapor_targets[n], gz))
 
     def await_vapor(step, X):
         slots = vapor_slots(X)
         for n in range(8):
-            arrive(slots[n], us_sem.at[step, n], ur_sem.at[step, n])
+            arrive(slots[n], us_sem.at[step, n], ur_sem.at[step, n],
+                   -vapor_targets[n][0], -vapor_targets[n][1])
 
     lane8 = iota((8, 128), 1)
     sub8 = iota((8, 128), 0)
@@ -178,11 +206,12 @@
     def send_z(step):
         for n in range(5):
             send(ZS.at[step], ZR.at[step, n], zs_sem.at[step, n], zr_sem.at[step, n],
-                 dev(*z_targets[n], other))
+                 (*z_targets[n], other))
 
     def await_z(step):
         for n in range(5):
-            arrive(ZR.at[step, n], zs_sem.at[step, n], zr_sem.at[step, n])
+            arrive(ZR.at[step, n], zs_sem.at[step, n], zr_sem.at[step, n],
+                   -z_targets[n][0], -z_targets[n][1])
 
     edge_keep = lax.rem(lane8 + 2 * gz, 128) < 2
 
@@ -357,16 +386,17 @@
                     slot = block * 3 + 1 - ty
                     same = 1 if z is gz else 0
                     n = (6 if near else 0) + (ty + 1) * 2 + same
-                    send(SS, SR.at[slot], ss_sem.at[n], sr_sem.at[slot], dev(tx, ty, z))
+                    send(SS, SR.at[slot], ss_sem.at[n], sr_sem.at[slot], (tx, ty, z))
 
     def await_surface():
         for slot in range(12):
             if slot in (4, 7):
                 @pl.when(own_slot != slot)
                 def _():
-                    arrive(SR.at[slot], ss_sem.at[0], sr_sem.at[slot])
+                    arrive(SR.at[slot], ss_sem.at[0], sr_sem.at[slot], 0, 0)
             else:
-                arrive(SR.at[slot], ss_sem.at[0], sr_sem.at[slot])
+                arrive(SR.at[slot], ss_sem.at[0], sr_sem.at[slot],
+                       (-1, 0, 0, 1)[slot // 3], slot % 3 - 1)
 
     def assemble_surface():
         SK[0:8, :] = jnp.zeros((8, 128), F32)
@@ -464,16 +494,17 @@
         @pl.when(gz == 0)
         def _():
             for n in range(17):
-                p_copy(step, n).start()
+                when(exists(*p_targets[n][:2]), lambda: p_copy(step, n).start())
 
     def await_pressures(step):
         for slot in range(9):
             if slot == 4:
                 @pl.when(gz == 1)
                 def _():
-                    arrive(PR.at[step, slot], ps_sem.at[step, 0], pr_sem.at[step, slot])
+                    arrive(PR.at[step, slot], ps_sem.at[step, 0], pr_sem.at[step, slot], 0, 0)
             else:
-                arrive(PR.at[step, slot], ps_sem.at[step, 0], pr_sem.at[step, slot])
+                arrive(PR.at[step, slot], ps_sem.at[step, 0], pr_sem.at[step, slot],
+                       slot // 3 - 1, slot % 3 - 1)
 
     def coarse_pressure(step):
         blocks = []
@@ -511,35 +542,38 @@
     dn_row, up_row = -(1 - gz), gz
 
     def bulk_slots(X):
-        slots = [X.at[0:2, 8:40], X.at[10:12, 8:40], X.at[2:10, 0:8], X.at[2:10, 40:48]]
+        slots = [X.at[0:2, 8:40], X.at[10:12, 8:40], X.at[2:10, 6:8], X.at[2:10, 40:42]]
         for r in (1, 10):
-            for c in (0, 40):
-                slots.append(X.at[r:r + 1, c:c + 8])
+            for c in (7, 40):
+                slots.append(X.at[r:r + 1, c:c + 1])
         return slots
 
     def bulk_sources(X, r0, c0):
         def own(r, nr, c, nc):
             return X.at[r0 + r:r0 + r + nr, c0 + c:c0 + c + nc]
 
-        sources = [own(6, 2, 0, 32), own(0, 2, 0, 32), own(0, 8, 24, 8), own(0, 8, 0, 8)]
+        sources = [own(6, 2, 0, 32), own(0, 2, 0, 32), own(0, 8, 30, 2), own(0, 8, 0, 2)]
         for r in (7, 0):
-            for c in (24, 0):
-                sources.append(own(r, 1, c, 8))
+            for c in (31, 0):
+                sources.append(own(r, 1, c, 1))
         return sources
 
+    bulk_targets = [(up_row, 0, other), (dn_row, 0, other), (0, 1, gz), (0, -1, gz)]
+    bulk_origins = [(dn_row, 0), (up_row, 0), (0, -1), (0, 1)]
+    for tx, ox in ((up_row, dn_row), (dn_row, up_row)):
+        for ty in (1, -1):
+            bulk_targets.append((tx, ty, other))
+            bulk_origins.append((ox, -ty))
+
     def send_bulk(kind, X, r0, c0, D):
-        targets = [dev(up_row, 0, other), dev(dn_row, 0, other), dev(0, 1, gz), dev(0, -1, gz)]
-        for tx in (up_row, dn_row):
-            for ty in (1, -1):
-                targets.append(dev(tx, ty, other))
         sources, slots = bulk_sources(X, r0, c0), bulk_slots(D)
         for n in range(8):
-            send(sources[n], slots[n], bs_sem.at[kind, n], br_sem.at[kind, n], targets[n])
+            send(sources[n], slots[n], bs_sem.at[kind, n], br_sem.at[kind, n], bulk_targets[n])
 
     def await_bulk(kind, D):
         slots = bulk_slots(D)
         for n in range(8):
-            arrive(slots[n], bs_sem.at[kind, n], br_sem.at[kind, n])
+            arrive(slots[n], bs_sem.at[kind, n], br_sem.at[kind, n], *bulk_origins[n])
 
     def clear_bulk(X):
         @pl.when(row_block == 0)
@@ -597,7 +631,7 @@
             else:
                 dst[r] = new
 
-    pl.semaphore_wait(barrier, 17)
+    pl.semaphore_wait(barrier, 2 * beside_x * beside_y - 1)
     send_vapor(0, lambda x, n, y, m: u_hbm.at[:, x:x + n, y:y + m], A)
     loads[0].wait()
     pack_z(0, A)
@@ -620,14 +654,14 @@
         B[c, x + 2, 8:24, :] = v
 
     advance(A, to_b)
+    pressures(0, B, 2, 8)
+    send_pressures(0)
+    pack_z(1, B)
+    send_z(1)
     first = len(sent)
     send_vapor(1, lambda x, n, y, m: B.at[:, x + 2:x + 2 + n, y + 8:y + 8 + m], B)
     sent_b = sent[first:]
     del sent[first:]
-    pressures(0, B, 2, 8)
-    send_pressures(0)
-    pack_z(1, B)
-    send_z(1)
 
     await_surface()
     assemble_surface()
@@ -651,8 +685,7 @@
     unpack_z(1)
     await_vapor(1, B)
     clear_outside(B)
-    for copy in sent_b:
-        copy.wait_send()
+    drain(sent_b)
     lane32 = iota((32, 128), 1)
     height = (lane32 + gz * 128).astype(F32)
     height_edge = (lane32 + other * 128).astype(F32)
@@ -714,14 +747,13 @@
         deep = TA[2 + 4 * half:6 + 4 * half, 8:40, :]
         to_ref[4 * half:4 * half + 4] = jnp.where(shallow, turned, deep)
 
-    for copy in sent:
-        copy.wait_send()
+    drain(sent)
 
     @pl.when(gz == 0)
     def _():
         for step in range(2):
             for n in range(17):
-                p_copy(step, n).wait_send()
+                when(exists(*p_targets[n][:2]), lambda: p_copy(step, n).wait_send())
 
 
 def solution(mesh):

time: 45.1 us -> 36.2 us (0.80)
  the two profiles are of different devices: /device:TPU:1 before, /device:TPU:24 now
where the time goes in v3:
time: 36.2 us; the launch traced here: 35.8 us
  Pallas kernels  33.8 us (93%)
  local copies, waits for them, and re-layouts  1.4 us (4%)
  between operations  0.64 us (2%)
    pallas_call x1, Pallas kernels, shards(): pl.pallas_call(functools.partial(kernel, sizes), out_shape=(pltpu.VMEM((6...  33.8 us
    unnamed x2, local copies, waits for them, and re-layouts  1.4 us

profile of v3, /device:TPU:24, one launch (start us, length us, event | category | flops | bytes accessed | tf_op | source)
XLA Modules:
  0.0 35.8 jit_solution(12567064547873904173)
XLA Ops:
  0.6 33.8 %shard_map.68 = (f32[6,8,16,128]{3,2,1,0:T(8,128)S(1)}, f32[8,32,128]{2,1,0:T(8,128)S(1)}) custom-call(f32[6,8,16,128]{3,2,1,0:T(8,128)} %u_hbm.1, f32[8,32,128]{2,1,0:T(8,128)} %bitcast.5, s32[8,32,128]{2,1,0:T(8,128)} %bitcast.6, s32[8,16]{1,0:T(8,128)} %lvl_ref.1, s32[2,4]{1,0:T(2,128)} %bitcast.7), custom_call_target="tpu_custom_call" | custom-call | tf_op jit(solution)/shard_map/pallas_call | solution.py:767
  34.4 0.7 %copy.9 = f32[6,8,16,128]{3,2,1,0:T(8,128)} copy(f32[6,8,16,128]{3,2,1,0:T(8,128)S(1)} %get-tuple-element.6) | data formatting | bytes 786432
  35.2 0.7 %copy.10 = f32[128,8,32]{0,2,1:T(8,128)} copy(f32[128,8,32]{0,2,1:T(8,128)S(1)} %bitcast.4) | data formatting | bytes 262144

commit v4 on v3

--- a/solution.py
+++ b/solution.py
@@ -41,7 +41,7 @@
     return lax.broadcasted_iota(jnp.int32, shape, dim)
 
 
-def forward_euler(load, edge):
+def forward_euler(load, edge, which=range(6)):
     def vertical(c):
         center, other = load(c, 0, 0), edge(c)
         lane = iota(center.shape, 1)
@@ -63,8 +63,8 @@
         -0.15 * (p_up - p_dn),
         -0.15 * spread,
     )
-    out = []
-    for c in range(6):
+    out = {}
+    for c in which:
         if c == 4:
             up, dn = w_up, w_dn
         elif c == 5:
@@ -72,7 +72,7 @@
         else:
             up, dn = vertical(c)
         sides = (load(c, 1, 0) + load(c, -1, 0)) + (load(c, 0, 1) + load(c, 0, -1))
-        out.append(
+        out[c] = (
             BASE[c] * load(c, 0, 0) + SIDE[c] * sides + UPC[c] * up + DNC[c] * dn + coupled[c]
         )
     return out
@@ -273,7 +273,7 @@
                     UE[c, xi, 0:8, :] = rim
                     UE[c, xi, 24:32, :] = rim
 
-    def advance(X, emit):
+    def advance(X, emit, early=None):
         rim_rows = rim_flags()
         lane16 = iota((16, 128), 1)
         edge_lane = jnp.where(gz == 0, 0, 127)
@@ -316,14 +316,22 @@
         def _():
             F[:, 9:10] = jnp.zeros((6, 1, 32, 128), F32)
 
-        @pl.loop(0, 8, unroll=2)
-        def _(x):
-            def load(c, dx, dy):
-                return F[c, x + 1 + dx, 8 + dy:24 + dy, :]
-
-            new = forward_euler(load, lambda c: FE[c, x])
-            for c in range(6):
-                emit(c, x, 0.5 * (X[c, x + 2, 8:24, :] + new[c]))
+        def second(which, count):
+            @pl.loop(0, 8, unroll=count)
+            def _(x):
+                def load(c, dx, dy):
+                    return F[c, x + 1 + dx, 8 + dy:24 + dy, :]
+
+                new = forward_euler(load, lambda c: FE[c, x], which)
+                for c in which:
+                    emit(c, x, 0.5 * (X[c, x + 2, 8:24, :] + new[c]))
+
+        if early is None:
+            second(range(6), 2)
+        else:
+            second((5,), 4)
+            early()
+            second(range(5), 2)
 
     row_first = gx * 16 - 8
     col_first = gy * 32 - 32
@@ -482,6 +490,10 @@
     p_targets = [(tx, ty, s) for tx in (-1, 0, 1) for ty in (-1, 0, 1) for s in (0, 1)
                  if (tx, ty, s) != (0, 0, 1)]
 
+    def p_needed(step, n):
+        tx, ty, same = p_targets[n]
+        return step == 0 or (not (tx and ty) and (same or tx != 1))
+
     def p_copy(step, n):
         tx, ty, s = p_targets[n]
         slot = (1 - tx) * 3 + 1 - ty
@@ -494,7 +506,8 @@
         @pl.when(gz == 0)
         def _():
             for n in range(17):
-                when(exists(*p_targets[n][:2]), lambda: p_copy(step, n).start())
+                if p_needed(step, n):
+                    when(exists(*p_targets[n][:2]), lambda: p_copy(step, n).start())
 
     def await_pressures(step):
         for slot in range(9):
@@ -502,7 +515,11 @@
                 @pl.when(gz == 1)
                 def _():
                     arrive(PR.at[step, slot], ps_sem.at[step, 0], pr_sem.at[step, slot], 0, 0)
-            else:
+            elif step == 1 and slot == 1:
+                @pl.when((gz == 0) & (gx > 0))
+                def _():
+                    arrive(PR.at[step, slot], ps_sem.at[step, 0], pr_sem.at[step, slot], 0, 0)
+            elif step == 0 or slot in (3, 5, 7):
                 arrive(PR.at[step, slot], ps_sem.at[step, 0], pr_sem.at[step, slot],
                        slot // 3 - 1, slot % 3 - 1)
 
@@ -653,9 +670,11 @@
     def to_b(c, x, v):
         B[c, x + 2, 8:24, :] = v
 
-    advance(A, to_b)
-    pressures(0, B, 2, 8)
-    send_pressures(0)
+    def share_first():
+        pressures(0, B, 2, 8)
+        send_pressures(0)
+
+    advance(A, to_b, share_first)
     pack_z(1, B)
     send_z(1)
     first = len(sent)
@@ -707,9 +726,11 @@
     def to_out(c, x, v):
         uo_ref[c, x] = v
 
-    advance(B, to_out)
-    pressures(1, uo_ref, 0, 0)
-    send_pressures(1)
+    def share_pressure():
+        pressures(1, uo_ref, 0, 0)
+        send_pressures(1)
+
+    advance(B, to_out, share_pressure)
 
     await_bulk(2, TB)
     clear_bulk(TB)
@@ -753,7 +774,19 @@
     def _():
         for step in range(2):
             for n in range(17):
-                when(exists(*p_targets[n][:2]), lambda: p_copy(step, n).wait_send())
+                if p_needed(step, n):
+                    when(exists(*p_targets[n][:2]), lambda: p_copy(step, n).wait_send())
+
+
+def write_back(gas_ref, temp_ref, gas_out, temp_out, sem):
+    copies = [
+        pltpu.make_async_copy(gas_ref, gas_out, sem.at[0]),
+        pltpu.make_async_copy(temp_ref, temp_out, sem.at[1]),
+    ]
+    for copy in copies:
+        copy.start()
+    for copy in copies:
+        copy.wait()
 
 
 def solution(mesh):
@@ -795,6 +828,18 @@
             ],
             compiler_params=pltpu.CompilerParams(collective_id=0, has_side_effects=True),
         )(vapor, jnp.transpose(thermal, (1, 2, 0)), jnp.transpose(phase, (1, 2, 0)), level, path.T)
+        gas = pltpu.with_memory_space_constraint(gas, pltpu.VMEM)
+        temp = pltpu.with_memory_space_constraint(temp, pltpu.VMEM)
+        gas, temp = pl.pallas_call(
+            write_back,
+            out_shape=(
+                jax.ShapeDtypeStruct((6, 8, 16, 128), F32),
+                jax.ShapeDtypeStruct((8, 32, 128), F32),
+            ),
+            in_specs=[vmem, vmem],
+            out_specs=(anywhere, anywhere),
+            scratch_shapes=[dma((2,))],
+        )(gas, temp)
         return gas, jnp.transpose(temp, (2, 0, 1))
 
     return jax.shard_map(

time: 36.2 us -> 34.9 us (0.964)
  local copies, waits for them, and re-layouts: 1.4 us -> 0 us
    unnamed x2 -> x0, local copies, waits for them, and re-layouts: 1.4 us -> none
    pallas_call x0 -> x1, Pallas kernels: none -> 0.8 us  [shards(): pl.pallas_call(write_back, out_shape=(jax.ShapeDtypeStruct((6, 8, 16, 128...]
    pallas_call x1, Pallas kernels: 33.8 us -> 33.3 us  [shards(): pl.pallas_call(functools.partial(kernel, sizes), out_shape=(pltpu.VMEM((6...]
where the time goes in v4:
time: 34.9 us; the launch traced here: 34.7 us
  Pallas kernels  34.1 us (98%)
  between operations  0.64 us (2%)
    pallas_call x1, Pallas kernels, shards(): pl.pallas_call(functools.partial(kernel, sizes), out_shape=(pltpu.VMEM((6...  33.3 us
    pallas_call x1, Pallas kernels, shards(): pl.pallas_call(write_back, out_shape=(jax.ShapeDtypeStruct((6, 8, 16, 128...  0.8 us

profile of v4, /device:TPU:24, one launch (start us, length us, event | category | flops | bytes accessed | tf_op | source)
XLA Modules:
  0.0 34.7 jit_solution(13878315975015507151)
XLA Ops:
  0.6 33.3 %shard_map.68 = (f32[6,8,16,128]{3,2,1,0:T(8,128)S(1)}, f32[8,32,128]{2,1,0:T(8,128)S(1)}) custom-call(f32[6,8,16,128]{3,2,1,0:T(8,128)} %u_hbm.1, f32[8,32,128]{2,1,0:T(8,128)} %bitcast.4, s32[8,32,128]{2,1,0:T(8,128)} %bitcast.5, s32[8,16]{1,0:T(8,128)} %lvl_ref.1, s32[2,4]{1,0:T(2,128)} %bitcast.6), custom_call_target="tpu_custom_call" | custom-call | tf_op jit(solution)/shard_map/pallas_call | solution.py:800
  33.9 0.8 %shard_map.69 = (f32[6,8,16,128]{3,2,1,0:T(8,128)}, f32[8,32,128]{2,1,0:T(8,128)}) custom-call(f32[6,8,16,128]{3,2,1,0:T(8,128)S(1)} %get-tuple-element.6.gas_ref, f32[8,32,128]{2,1,0:T(8,128)S(1)} %get-tuple-element.7.temp_ref), custom_call_target="tpu_custom_call" | custom-call | tf_op jit(solution)/shard_map/pallas_call | solution.py:833

commit v5 on v4

--- a/solution.py
+++ b/solution.py
@@ -84,7 +84,7 @@
     uo_ref, to_ref,
     A, B, F, UE, FE, ZS, ZR, SS, SR, PS, PR,
     TA, MA, TB, TC, KB, GX, GY, GD, LXB, LYD,
-    SA, SB, SK, SGX, SGY, SGD, SGB, SL, SM, LO, LL, MM,
+    SA, SB, SK, SGX, SGY, SGD, SGB, SL, SM, HIT, LL, MM,
     in_sem, us_sem, ur_sem, zs_sem, zr_sem, ss_sem, sr_sem, ps_sem, pr_sem,
     bs_sem, br_sem,
 ):
@@ -371,7 +371,10 @@
             [lvl_ref[...].astype(F32), jnp.zeros((8, 112), F32)], axis=1)
         SS[4] = level
         eye = jnp.where(iota((16, 128), 0) == iota((16, 128), 1), 1.0, 0.0)
-        LO[...] = nt(eye, jnp.concatenate([level, jnp.zeros((120, 128), F32)], axis=0))
+        own = nt(eye, jnp.concatenate([level, jnp.zeros((120, 128), F32)], axis=0))
+        heights = (iota((16, 128), 1) + gz * 128).astype(F32)
+        for x in range(8):
+            HIT[x] = jnp.where(heights == own[:, x:x + 1], 1.0, 0.0)
 
     def pack_surface():
         pick = jnp.where(sub8 == lane8, 1.0, 0.0)
@@ -452,7 +455,7 @@
         eye = jnp.where(iota((48, 128), 0) == iota((48, 128), 1), 1.0, 0.0)
         LL[...] = nt(eye, jnp.concatenate(blocks, axis=0))
 
-    def surface_substep(sub, src, dst, fine_pressure):
+    def surface_conduct(sub, src, dst):
         for chunk in range(4):
             base = chunk * 64
             t = src[base + 8:base + 72, :]
@@ -467,6 +470,8 @@
             change = change + (flow3 - pltpu.roll(flow3, 1, 1)).reshape(64, 128)
             change = change - SGB[base:base + 64, :] * t + SL[sub, base:base + 64, :]
             dst[base + 8:base + 72, :] = (t + change) * SM[base:base + 64, :]
+
+    def surface_cool(src, dst, fine_pressure):
         top = src[pl.ds(8, 32, stride=8), :]
         cooling = LATENT_HEAT * softplus(top - 1.0 - 0.5 * fine_pressure)
         cooling = cooling * SM[pl.ds(0, 32, stride=8), :]
@@ -474,12 +479,10 @@
 
     def pressures(step, X, at_x, at_y):
         lane16 = iota((16, 128), 1)
-        height = (lane16 + gz * 128).astype(F32)
         acc = jnp.zeros((16, 128), F32)
         for x in range(8):
             v = X[5, x + at_x, at_y:at_y + 16, :]
-            hit = height == LO[:, x:x + 1]
-            s = jnp.sum(jnp.where(hit, v, 0.0), axis=1, keepdims=True)
+            s = jnp.sum(HIT[x] * v, axis=1, keepdims=True)
             acc = jnp.where(lane16 == x, s, acc)
         PS[step] = acc
 
@@ -692,13 +695,15 @@
     bulk_substep(1, TC, TB, 2, 10, True)
     send_bulk(2, TB, 2, 8, TB)
 
+    surface_conduct(0, SA, SB)
+    LL[0:32, :] = with_rim(LL[...])
     await_pressures(0)
     coarse = coarse_pressure(0)
     fine = fine_from_coarse(coarse)
-    surface_substep(0, SA, SB, fine)
-    surface_substep(1, SB, SA, fine)
+    surface_cool(SA, SB, fine)
+    surface_conduct(1, SB, SA)
+    surface_cool(SB, SA, fine)
     MM[...] = with_rim(mass_from_surface(SA, coarse))
-    LL[0:32, :] = with_rim(LL[...])
 
     await_z(1)
     unpack_z(1)
@@ -708,20 +713,26 @@
     lane32 = iota((32, 128), 1)
     height = (lane32 + gz * 128).astype(F32)
     height_edge = (lane32 + other * 128).astype(F32)
-    for xi in range(12):
+    def field_at(xi, heights):
         mass = jnp.broadcast_to(MM[:, xi + 6:xi + 7], (32, 128))
         level = jnp.broadcast_to(LL[0:32, xi + 6:xi + 7], (32, 128))
-        field = jnp.where(height == level, mass, 0.0)
-        B[0, xi] = B[0, xi] + 0.5 * field
-        B[4, xi] = B[4, xi] + 0.4 * field
-        B[5, xi] = B[5, xi] + 0.6 * field
-        if 1 <= xi <= 10:
-            @pl.when(gz == 1)
-            def _():
-                edge = jnp.where((height_edge == level) & (lane32 >= 126), mass, 0.0)
-                UE[0, xi - 1] = UE[0, xi - 1] + 0.5 * edge
-                UE[4, xi - 1] = UE[4, xi - 1] + 0.4 * edge
-                UE[5, xi - 1] = UE[5, xi - 1] + 0.6 * edge
+        return jnp.where(heights == level, mass, 0.0)
+
+    @pl.when(gz == 0)
+    def _():
+        for xi in range(12):
+            field = field_at(xi, height)
+            B[0, xi] = B[0, xi] + 0.5 * field
+            B[4, xi] = B[4, xi] + 0.4 * field
+            B[5, xi] = B[5, xi] + 0.6 * field
+
+    @pl.when(gz == 1)
+    def _():
+        for xi in range(1, 11):
+            field = jnp.where(lane32 >= 126, field_at(xi, height_edge), 0.0)
+            UE[0, xi - 1] = UE[0, xi - 1] + 0.5 * field
+            UE[4, xi - 1] = UE[4, xi - 1] + 0.4 * field
+            UE[5, xi - 1] = UE[5, xi - 1] + 0.6 * field
 
     def to_out(c, x, v):
         uo_ref[c, x] = v
@@ -737,18 +748,17 @@
     bulk_substep(2, TB, TC, 1, 11)
     bulk_substep(3, TC, TA, 2, 10, True)
 
+    surface_conduct(2, SA, SB)
     await_pressures(1)
     coarse = coarse_pressure(1)
     fine = fine_from_coarse(coarse)
-    surface_substep(2, SA, SB, fine)
-    surface_substep(3, SB, SA, fine)
+    surface_cool(SA, SB, fine)
+    surface_conduct(3, SB, SA)
+    surface_cool(SB, SA, fine)
     mass_now = mass_from_surface(SA, coarse)[16:32]
-    lane16 = iota((16, 128), 1)
-    height = (lane16 + gz * 128).astype(F32)
     for x in range(8):
         mass = jnp.broadcast_to(mass_now[:, x + 8:x + 9], (16, 128))
-        level = jnp.broadcast_to(LO[:, x:x + 1], (16, 128))
-        field = jnp.where(height == level, mass, 0.0)
+        field = HIT[x] * mass
         uo_ref[0, x] = uo_ref[0, x] + 0.5 * field
         uo_ref[4, x] = uo_ref[4, x] + 0.4 * field
         uo_ref[5, x] = uo_ref[5, x] + 0.6 * field
@@ -820,7 +830,7 @@
                 pltpu.VMEM((272, 128), F32), pltpu.VMEM((264, 128), F32),
                 pltpu.VMEM((256, 128), F32), pltpu.VMEM((256, 128), F32),
                 pltpu.VMEM((256, 128), F32), pltpu.VMEM((4, 256, 128), F32),
-                pltpu.VMEM((256, 128), F32), pltpu.VMEM((16, 128), F32),
+                pltpu.VMEM((256, 128), F32), pltpu.VMEM((8, 16, 128), F32),
                 pltpu.VMEM((48, 128), F32), pltpu.VMEM((32, 128), F32),
                 dma((3,)), dma((2, 8)), dma((2, 8)), dma((2, 5)), dma((2, 5)),
                 dma((12,)), dma((12,)), dma((2, 17)), dma((2, 9)),

time: 34.9 us -> 33.8 us (0.968)
  Pallas kernels: 34.1 us -> 33 us
    pallas_call x1, Pallas kernels: 33.3 us -> 32.2 us  [shards(): pl.pallas_call(functools.partial(kernel, sizes), out_shape=(pltpu.VMEM((6...]
where the time goes in v5:
time: 33.8 us; the launch traced here: 33.7 us
  Pallas kernels  33 us (98%)
  between operations  0.64 us (2%)
    pallas_call x1, Pallas kernels, shards(): pl.pallas_call(functools.partial(kernel, sizes), out_shape=(pltpu.VMEM((6...  32.2 us
    pallas_call x1, Pallas kernels, shards(): pl.pallas_call(write_back, out_shape=(jax.ShapeDtypeStruct((6, 8, 16, 128...  0.8 us

profile of v5, /device:TPU:24, one launch (start us, length us, event | category | flops | bytes accessed | tf_op | source)
XLA Modules:
  0.0 33.7 jit_solution(793602213694871414)
XLA Ops:
  0.6 32.2 %shard_map.68 = (f32[6,8,16,128]{3,2,1,0:T(8,128)S(1)}, f32[8,32,128]{2,1,0:T(8,128)S(1)}) custom-call(f32[6,8,16,128]{3,2,1,0:T(8,128)} %u_hbm.1, f32[8,32,128]{2,1,0:T(8,128)} %bitcast.4, s32[8,32,128]{2,1,0:T(8,128)} %bitcast.5, s32[8,16]{1,0:T(8,128)} %lvl_ref.1, s32[2,4]{1,0:T(2,128)} %bitcast.6), custom_call_target="tpu_custom_call" | custom-call | tf_op jit(solution)/shard_map/pallas_call | solution.py:810
  32.9 0.8 %shard_map.69 = (f32[6,8,16,128]{3,2,1,0:T(8,128)}, f32[8,32,128]{2,1,0:T(8,128)}) custom-call(f32[6,8,16,128]{3,2,1,0:T(8,128)S(1)} %get-tuple-element.6.gas_ref, f32[8,32,128]{2,1,0:T(8,128)S(1)} %get-tuple-element.7.temp_ref), custom_call_target="tpu_custom_call" | custom-call | tf_op jit(solution)/shard_map/pallas_call | solution.py:843

commit v6 on v5

--- a/solution.py
+++ b/solution.py
@@ -278,7 +278,7 @@
         lane16 = iota((16, 128), 1)
         edge_lane = jnp.where(gz == 0, 0, 127)
 
-        @pl.loop(0, 10, unroll=2)
+        @pl.loop(0, 10, unroll=10)
         def _(i):
             xi = i + 1
 
@@ -289,7 +289,7 @@
             for c in range(6):
                 F[c, i, 8:24, :] = new[c]
 
-        @pl.loop(0, 8, unroll=2)
+        @pl.loop(0, 8, unroll=8)
         def _(x):
             def load_rim(c, dx, dy):
                 start = {0: 0, 1: 1, -1: 23}[dy]
@@ -327,11 +327,11 @@
                     emit(c, x, 0.5 * (X[c, x + 2, 8:24, :] + new[c]))
 
         if early is None:
-            second(range(6), 2)
+            second(range(6), 4)
         else:
-            second((5,), 4)
+            second((5,), 8)
             early()
-            second(range(5), 2)
+            second(range(5), 4)
 
     row_first = gx * 16 - 8
     col_first = gy * 32 - 32

time: 33.8 us -> 32.3 us (0.956)
  Pallas kernels: 33 us -> 31.5 us
    pallas_call x1, Pallas kernels: 32.2 us -> 30.7 us  [shards(): pl.pallas_call(functools.partial(kernel, sizes), out_shape=(pltpu.VMEM((6...]
where the time goes in v6:
time: 32.3 us; the launch traced here: 32.2 us
  Pallas kernels  31.5 us (98%)
  between operations  0.64 us (2%)
    pallas_call x1, Pallas kernels, shards(): pl.pallas_call(functools.partial(kernel, sizes), out_shape=(pltpu.VMEM((6...  30.7 us
    pallas_call x1, Pallas kernels, shards(): pl.pallas_call(write_back, out_shape=(jax.ShapeDtypeStruct((6, 8, 16, 128...  0.8 us

profile of v6, /device:TPU:24, one launch (start us, length us, event | category | flops | bytes accessed | tf_op | source)
XLA Modules:
  0.0 32.2 jit_solution(12885520042470781613)
XLA Ops:
  0.6 30.7 %shard_map.68 = (f32[6,8,16,128]{3,2,1,0:T(8,128)S(1)}, f32[8,32,128]{2,1,0:T(8,128)S(1)}) custom-call(f32[6,8,16,128]{3,2,1,0:T(8,128)} %u_hbm.1, f32[8,32,128]{2,1,0:T(8,128)} %bitcast.4, s32[8,32,128]{2,1,0:T(8,128)} %bitcast.5, s32[8,16]{1,0:T(8,128)} %lvl_ref.1, s32[2,4]{1,0:T(2,128)} %bitcast.6), custom_call_target="tpu_custom_call" | custom-call | tf_op jit(solution)/shard_map/pallas_call | solution.py:810
  31.4 0.8 %shard_map.69 = (f32[6,8,16,128]{3,2,1,0:T(8,128)}, f32[8,32,128]{2,1,0:T(8,128)}) custom-call(f32[6,8,16,128]{3,2,1,0:T(8,128)S(1)} %get-tuple-element.6.gas_ref, f32[8,32,128]{2,1,0:T(8,128)S(1)} %get-tuple-element.7.temp_ref), custom_call_target="tpu_custom_call" | custom-call | tf_op jit(solution)/shard_map/pallas_call | solution.py:843
